TPU v7x, 32 devices: a whole 2x2x4 slice. The times are simulated.
32 devices in a mesh: blk: 16 (over z, y, x), sub: 2 (over core).
Axes of the slice: x: 2, y: 2, z: 4, core: 2. Of those that a mesh axis runs over, the one named last changes fastest.
Arguments:
- velocity: float32 [3, 1190112], P(None, ('blk', 'sub')), may hold values from -4 to 4, as said below
- pressure_load: float32 [1190112], P(('blk', 'sub')), may hold values from -24 to 24, as said below
- local_map: int32 [216, 8192], P(None, ('blk', 'sub')), may hold values from 0 to 37190, as said below
- stiff_geo: float32 [3, 8192], P(None, ('blk', 'sub')), may hold values from 0.1 to 1
- mass_geo: float32 [8192], P(('blk', 'sub')), may hold values from 1 to 10
Outputs:
- vel_applied: float32 [3, 1190112], P(None, ('blk', 'sub'))
- pressure: float32 [1190112], P(('blk', 'sub'))
- new_residual: float32 [1190112], P(('blk', 'sub'))
Inputs may be any that keep to these rules, and one draw needn't show every extreme that they name: `velocity`: copies of one node stored on neighbouring devices hold equal values. `pressure_load`: copies of one node stored on neighbouring devices hold equal values. `local_map`: the 256 columns of each device name that device's 2 x 4 x 32 elements, each once, in any order; the element at position (ex, ez, ey) lists for node n = 36 i + 6 j + k the local index ((5 ex + i) * 21 + 5 ez + j) * 161 + 5 ey + k.
All inputs are finite; a program needn't handle non-finite values.
Results may differ from a plain program's by a relative error of at most 0.0003.
The roundings to bfloat16 on the way count: a program that leaves them out, or rounds other values in their place, can miss the bound.
Values sent between devices are 32-bit elements; how exact they have to be, the bound alone decides.
A program may use at most 64 MiB of HBM per device.

v0:
```python
import functools
import math

import jax
import jax.numpy as jnp
import numpy as np
from jax import lax
from jax.experimental import pallas as pl
from jax.experimental.pallas import tpu as pltpu
from jax.sharding import PartitionSpec as P

EX = 2
EZ = 4
EY = 32
CHEB_ITERS = 8
NX = 5 * EX + 1
NZ = 5 * EZ + 1
NY = 5 * EY + 1
NLOC = NX * NZ * NY
NZP = 24
NYP = 256
REACH = -(-(CHEB_ITERS - 1) // EZ)
SPAN = 2 * REACH + 1
NZV = SPAN * EZ + 1
EXCH = 8
ZT = -(-NX // 4)
LAST = (NX - 1) % 4

DAMPING = 0.3
MASS_SHARE = 0.05
SPECTRUM_LOW = 0.15
SPECTRUM_HIGH = 4.5
MESH = pl.DeviceIdType.MESH
F32 = jnp.float32
BF16 = jnp.bfloat16


def tables():
    seven_root = math.sqrt(7.0)
    inner = math.sqrt(1.0 / 3.0 - 2.0 * seven_root / 21.0)
    outer = math.sqrt(1.0 / 3.0 + 2.0 * seven_root / 21.0)
    xi = np.array([-1.0, -outer, -inner, inner, outer, 1.0])
    leg = (63.0 * xi**5 - 70.0 * xi**3 + 15.0 * xi) / 8.0
    w = 2.0 / (30.0 * leg**2)
    D = np.zeros((6, 6))
    for i in range(6):
        for j in range(6):
            if i != j:
                D[i, j] = leg[i] / (leg[j] * (xi[i] - xi[j]))
    D[0, 0] = -7.5
    D[5, 5] = 7.5
    k1 = D.T @ (w[:, None] * D)
    lin = np.stack([(1.0 - xi) / 2.0, (1.0 + xi) / 2.0], 1)
    kc = lin.T @ k1 @ lin
    mc = lin.T @ (w[:, None] * lin)
    coarse = [
        np.kron(np.kron(kc, mc), mc),
        np.kron(np.kron(mc, kc), mc),
        np.kron(np.kron(mc, mc), kc),
        MASS_SHARE * np.kron(np.kron(mc, mc), mc),
    ]
    return D, w, k1, lin, coarse


def roll_tables(M):
    out = np.zeros((8, 8, 128), np.float32)
    for s in range(8):
        for j in range(6):
            m = (j - s) % 8
            if m < 6:
                out[s, j, :] = M[j, m]
    return out


def col_tile(values):
    tile = np.zeros((1, 8, 128), np.float32)
    tile[0, :6, :] = np.asarray(values)[:, None]
    return tile


def bf16_round(a):
    return np.asarray(a, np.float32).astype(np.dtype(BF16)).astype(np.float64)


def pick_matrices():
    pick = np.zeros((NYP, 6, 128), np.float32)
    put = np.zeros((6, 128, NYP), np.float32)
    for k in range(6):
        for z in range(EZ):
            for e in range(EY):
                pick[5 * e + k, k, z * EY + e] = 1.0
                if k < 5 or e == EY - 1:
                    put[k, z * EY + e, 5 * e + k] = 1.0
    return pick.reshape(NYP, 768), put.reshape(768, NYP)


def mac(pairs):
    total = None
    for coef, value in pairs:
        if isinstance(coef, (float, int)) and coef == 0.0:
            continue
        term = coef * value
        total = term if total is None else total + term
    return total


def kernel(
    n_blk,
    n_sub,
    xs,
    vel_ref,
    load_ref,
    map_hbm,
    stiff_ref,
    mass_ref,
    tab_ref,
    pick_ref,
    put_ref,
    velout_ref,
    pres_ref,
    res_ref,
    V,
    W,
    FS,
    map_ref,
    R,
    INV,
    VV,
    VE,
    GX,
    GC,
    SG,
    xsend,
    xrecv,
    zsend,
    zrecv,
    drecv,
    csend,
    crecv,
    rsend,
    rrecv,
    CF,
    ST,
    CU,
    CR,
    psend,
    precv,
    ex_send,
    ex_recv,
    c_send,
    c_recv,
    p_sem,
    m_sem,
):
    D, w, k1, lin, coarse = tables()
    Dh = bf16_round(D)
    n_dev = n_blk * n_sub
    b = lax.axis_index("blk")
    s = lax.axis_index("sub")
    me = b * n_sub + s

    def device_of(linear):
        return (linear // n_sub, lax.rem(linear, n_sub))

    has = {
        "xl": s > 0,
        "xh": s < n_sub - 1,
        "zl": b > 0,
        "zh": b < n_blk - 1,
    }

    def zero(ref_slice):
        ref_slice[...] = jnp.zeros(ref_slice.shape, F32)

    for side, name in ((0, "xl"), (1, "xh")):

        @pl.when(jnp.logical_not(has[name]))
        def _(side=side):
            zero(xrecv.at[:, side])

    for side, name in ((0, "zl"), (1, "zh")):

        @pl.when(jnp.logical_not(has[name]))
        def _(side=side):
            zero(zrecv.at[:, side])

    for zs, zname in ((0, "zl"), (1, "zh")):
        for xside, xname in ((0, "xl"), (1, "xh")):

            @pl.when(jnp.logical_not(jnp.logical_and(has[zname], has[xname])))
            def _(zs=zs, xside=xside):
                zero(drecv.at[:, zs, xside])

    for o in range(SPAN):
        off = o - REACH

        @pl.when(jnp.logical_or(b + off < 0, b + off >= n_blk))
        def _(o=o):
            zero(crecv.at[o])
            zero(rrecv.at[o])

    barrier = pltpu.get_barrier_semaphore()
    map_copy = pltpu.make_async_copy(map_hbm.at[0:8, :], map_ref, m_sem)
    map_copy.start()

    def greet(d, carry):
        pl.semaphore_signal(
            barrier, inc=1, device_id=device_of(lax.rem(me + d, n_dev)), device_id_type=MESH
        )
        return carry

    lax.fori_loop(1, n_dev, greet, 0)

    lane = lax.broadcasted_iota(jnp.int32, (8, 128), 1)
    sub_i = lax.broadcasted_iota(jnp.int32, (8, 128), 0)
    lane88 = lax.broadcasted_iota(jnp.int32, (8 * NX, 768), 1) // EY % EZ
    row88 = lax.broadcasted_iota(jnp.int32, (8 * NX, 768), 0) % 8
    CT = lambda q: tab_ref[q]
    WJ = tab_ref[24]
    LJ = (tab_ref[25], tab_ref[26])

    FS[...] = jnp.zeros(FS.shape, F32)

    def to_elements(field, dest, exact):
        FS[:, 0:NZ, 0:NY] = field[...]
        rows = jnp.concatenate(
            [FS[:, 5 * ez : 5 * ez + 8, :].reshape(8 * NX, NYP) for ez in range(EZ)], axis=0
        )
        hi = rows.astype(BF16)
        got = jnp.dot(hi, pick_ref[...], preferred_element_type=F32)
        if exact:
            lo = (rows - hi.astype(F32)).astype(BF16)
            got = got + jnp.dot(lo, pick_ref[...], preferred_element_type=F32)
        result = jnp.zeros((8 * NX, 768), F32)
        for ez in range(EZ):
            piece = got[8 * NX * ez : 8 * NX * (ez + 1)]
            result = jnp.where(jnp.logical_and(lane88 == ez, row88 < 6), piece, result)
        for k in range(6):
            dest[:, k] = result[:, 128 * k : 128 * k + 128].reshape(NX, 8, 128)

    def to_nodes(source, dest):
        full = jnp.concatenate([source[:, k].reshape(8 * NX, 128) for k in range(6)], axis=1)
        hi = full.astype(BF16).astype(F32)
        lo = full - hi
        his = [jnp.where(lane88 == ez, hi, 0.0) for ez in range(EZ)]
        los = [jnp.where(lane88 == ez, lo, 0.0) for ez in range(EZ)]
        got = jnp.dot(
            jnp.concatenate(his, axis=0).astype(BF16), put_ref[...], preferred_element_type=F32
        ) + jnp.dot(
            jnp.concatenate(los, axis=0).astype(BF16), put_ref[...], preferred_element_type=F32
        )
        for ez in range(EZ):
            piece = got[8 * NX * ez : 8 * NX * (ez + 1)].reshape(NX, 8, NYP)
            dest[:, 5 * ez : 5 * ez + 6, :] = piece[:, :6, :NY]

    map_copy.wait()
    corner = map_ref[0:1, :]
    slot = (corner // (NZ * NY) // 5 * EZ + corner // NY % NZ // 5) * EY + corner % NY // 5
    count = EX * EZ * EY
    hot = (
        lax.broadcasted_iota(jnp.int32, (count, count), 0)
        == jnp.broadcast_to(slot, (count, count))
    ).astype(F32)
    geo = jnp.concatenate(
        [stiff_ref[...], mass_ref[...], jnp.zeros((4, count), F32)], axis=0
    )
    part_hi = geo.astype(BF16).astype(F32)
    part_mid = (geo - part_hi).astype(BF16).astype(F32)
    part_lo = geo - part_hi - part_mid
    pack = jnp.concatenate([part_hi, part_mid, part_lo], axis=0).astype(BF16)
    got = lax.dot_general(
        pack, hot.astype(BF16), (((1,), (1,)), ((), ())), preferred_element_type=F32
    )
    sorted_geo = got[0:8] + got[8:16] + got[16:24]
    g = [
        [
            jnp.broadcast_to(sorted_geo[q : q + 1, 128 * ex : 128 * ex + 128], (8, 128))
            for ex in range(EX)
        ]
        for q in range(4)
    ]
    for q in range(4):
        for ex in range(EX):
            SG[q, ex] = g[q][ex]
    for ex in range(EX):
        GX[ex] = WJ * g[0][ex]
    for x in range(NX):
        share = [(ex, x - 5 * ex) for ex in range(EX) if 0 <= x - 5 * ex <= 5]
        GC[0, x] = WJ * mac([(float(w[i]), g[2][ex]) for ex, i in share])
        GC[1, x] = mac([(float(w[i]), g[1][ex]) for ex, i in share])
        GC[2, x] = WJ * mac([(float(MASS_SHARE * w[i]), g[3][ex]) for ex, i in share])
    stack = jnp.zeros((8, 128), F32)
    for q in range(4):
        for ex in range(EX):
            stack = jnp.where(sub_i == EX * q + ex, g[q][ex], stack)
    csend[...] = stack

    def diagonal_part():
        kj = tab_ref[27]
        for x in range(NX):
            share = [(ex, x - 5 * ex) for ex in range(EX) if 0 <= x - 5 * ex <= 5]
            gx = mac([(float(k1[i, i]), GX[ex]) for ex, i in share])
            gy, gz, gm = GC[0, x], GC[1, x], GC[2, x]
            base = gx + gz * kj + gm
            for k in range(6):
                W[x, k] = float(w[k]) * base + float(k1[k, k]) * gy

    def apply_part(src, dst):
        for ex in range(EX):
            gx = GX[ex]
            for k in range(6):
                vs = [src[5 * ex + m, k] for m in range(6)]
                gk = float(w[k]) * gx
                for i in range(6):
                    value = gk * mac([(float(k1[i, m]), vs[m]) for m in range(6)])
                    if i == 0 and ex > 0:
                        value = value + dst[5 * ex, k]
                    dst[5 * ex + i, k] = value
        for x in range(NX):
            gy, gz, gm = GC[0, x], GC[1, x], GC[2, x]
            vs = [src[x, m] for m in range(6)]
            for k in range(6):
                vk = vs[k]
                zterm = CT(0) * vk
                for sh in range(1, 8):
                    zterm = zterm + CT(sh) * pltpu.roll(vk, sh, 0)
                value = float(w[k]) * (gz * zterm + gm * vk)
                value = value + gy * mac([(float(k1[k, m]), vs[m]) for m in range(6)])
                dst[x, k] = dst[x, k] + value

    ey = lane % EY
    lane6 = lax.broadcasted_iota(jnp.int32, (6, 128), 1)

    def link(idx, slot_no, src, dst, device):
        return pltpu.make_async_remote_copy(
            src_ref=src,
            dst_ref=dst,
            send_sem=ex_send.at[idx, slot_no],
            recv_sem=ex_recv.at[idx, slot_no],
            device_id=device,
            device_id_type=MESH,
        )

    def links(idx):
        both = jnp.logical_and
        out = [
            (has["xl"], has["xh"], link(idx, 1, xsend.at[idx, 0], xrecv.at[idx, 1], (b, s - 1))),
            (has["xh"], has["xl"], link(idx, 0, xsend.at[idx, 1], xrecv.at[idx, 0], (b, s + 1))),
            (has["zl"], has["zh"], link(idx, 3, zsend.at[idx, 0], zrecv.at[idx, 1], (b - 1, s))),
            (has["zh"], has["zl"], link(idx, 2, zsend.at[idx, 1], zrecv.at[idx, 0], (b + 1, s))),
        ]
        for zs, db, zn, zr in ((0, -1, "zl", "zh"), (1, 1, "zh", "zl")):
            for xside, ds, xn, xr in ((0, -1, "xl", "xh"), (1, 1, "xh", "xl")):
                out.append(
                    (
                        both(has[zn], has[xn]),
                        both(has[zr], has[xr]),
                        link(
                            idx,
                            4 + 2 * (1 - zs) + (1 - xside),
                            zsend.at[idx, zs, (ZT - 1) * xside],
                            drecv.at[idx, 1 - zs, 1 - xside],
                            (b + db, s + ds),
                        ),
                    )
                )
        return out

    def exchange_start(idx, F):
        for x in range(NX):
            low, high = F[x, 0], F[x, 5]
            F[x, 0] = low + jnp.where(ey > 0, pltpu.roll(high, 1, 1), 0.0)
            F[x, 5] = high + jnp.where(ey < EY - 1, pltpu.roll(low, 127, 1), 0.0)
        xsend[idx, 0] = F[0]
        xsend[idx, 1] = F[NX - 1]
        group = lane6 // EY
        for t in range(ZT):
            low = high = jnp.zeros((6, 128), F32)
            for m in range(4):
                x = 4 * t + m
                if x >= NX:
                    continue
                z0, z5 = F[x, :, 0, :], F[x, :, 5, :]
                if m:
                    z0 = pltpu.roll(z0, EY * m, 1)
                if m < 3:
                    z5 = pltpu.roll(z5, EY * (m + 1), 1)
                low = jnp.where(group == m, z0, low)
                high = jnp.where(group == m, z5, high)
            zsend[idx, 0, t, 0:6, :] = low
            zsend[idx, 1, t, 0:6, :] = high
        for there, _, copy in links(idx):

            @pl.when(there)
            def _(copy=copy):
                copy.start()

    def exchange_end(idx, F):
        for _, here, copy in links(idx):

            @pl.when(here)
            def _(copy=copy):
                copy.wait_recv()

        F[0] = F[0] + xrecv[idx, 0]
        F[NX - 1] = F[NX - 1] + xrecv[idx, 1]
        for x in range(NX):
            z0, z5 = F[x, :, 0, :], F[x, :, 5, :]
            t, m = divmod(x, 4)

            def moved(tile, shift):
                return tile if shift % 128 == 0 else pltpu.roll(tile, shift % 128, 1)

            near = moved(zrecv[idx, 0, t, 0:6, :], -EY * m)
            far = moved(zrecv[idx, 1, t, 0:6, :], 128 - EY - EY * m)
            if x == 0:
                near = near + moved(drecv[idx, 0, 0, 0:6, :], -EY * LAST)
                far = far + moved(drecv[idx, 1, 0, 0:6, :], 128 - EY - EY * LAST)
            if x == NX - 1:
                near = near + drecv[idx, 0, 1, 0:6, :]
                far = far + moved(drecv[idx, 1, 1, 0:6, :], 128 - EY)
            F[x, :, 0, :] = z0 + jnp.where(lane6 < EY, near, pltpu.roll(z5, EY, 1))
            F[x, :, 5, :] = z5 + jnp.where(lane6 >= 128 - EY, far, pltpu.roll(z0, 128 - EY, 1))

    def exchange_sent(idx):
        for there, _, copy in links(idx):

            @pl.when(there)
            def _(copy=copy):
                copy.wait_send()

    def window_copies(which, src, dst):
        out = []
        for off in range(-REACH, REACH + 1):
            for ds in range(n_sub):
                if off == 0 and ds == 0:
                    continue
                peer_s = lax.rem(s + ds, n_sub)
                target = b + off
                sending = jnp.logical_and(target >= 0, target < n_blk)
                copy = pltpu.make_async_remote_copy(
                    src_ref=src,
                    dst_ref=dst.at[REACH - off, s],
                    send_sem=c_send.at[which, REACH + off, ds],
                    recv_sem=c_recv.at[which, REACH - off, s],
                    device_id=(target, peer_s),
                    device_id_type=MESH,
                )
                arrive = pltpu.make_async_remote_copy(
                    src_ref=src,
                    dst_ref=dst.at[REACH + off, peer_s],
                    send_sem=c_send.at[which, REACH + off, ds],
                    recv_sem=c_recv.at[which, REACH + off, peer_s],
                    device_id=(target, peer_s),
                    device_id_type=MESH,
                )
                out.append((sending, copy, arrive))
        return out

    def window_start(which, src, dst):
        for sending, copy, _ in window_copies(which, src, dst):

            @pl.when(sending)
            def _(copy=copy):
                copy.start()

    def window_wait(which, src, dst):
        for sending, _, arrive in window_copies(which, src, dst):

            @pl.when(sending)
            def _(arrive=arrive):
                arrive.wait_recv()

    def window_sent(which, src, dst):
        for sending, copy, _ in window_copies(which, src, dst):

            @pl.when(sending)
            def _(copy=copy):
                copy.wait_send()

    diagonal_part()
    to_elements(load_ref, R, True)
    crecv[REACH, s] = csend[...]

    pl.semaphore_wait(barrier, n_dev - 1)

    exchange_start(0, W)
    window_start(0, csend, crecv)

    def velocity(c, carry):
        to_elements(vel_ref.at[c], VE, False)
        out = VV.at[c]
        rounded = lambda value: value.astype(BF16).astype(F32)
        for ex in range(EX):
            gx = SG[0, ex]
            for k in range(6):
                vs = [VE[5 * ex + m, k] for m in range(6)]
                flux = []
                for i in range(6):
                    grad = mac([(float(Dh[i, m]), vs[m]) for m in range(6)])
                    flux.append(rounded(grad * (WJ * float(w[i] * w[k])) * gx))
                for i in range(6):
                    value = mac([(float(Dh[m, i]), flux[m]) for m in range(6)])
                    if i == 0 and ex > 0:
                        value = value + out[5 * ex, k]
                    out[5 * ex + i, k] = value
        for ex in range(EX):
            gz, gy, gm = SG[1, ex], SG[2, ex], SG[3, ex]
            for i in range(6):
                x = 5 * ex + i
                vs = [VE[x, m] for m in range(6)]
                flux = []
                for k in range(6):
                    grad = mac([(float(Dh[k, m]), vs[m]) for m in range(6)])
                    flux.append(rounded(grad * (WJ * float(w[i] * w[k])) * gy))
                for k in range(6):
                    vk = vs[k]
                    weight = WJ * float(w[i] * w[k])
                    value = mac([(float(Dh[m, k]), flux[m]) for m in range(6)])
                    grad = tab_ref[8] * vk
                    for sh in range(1, 8):
                        grad = grad + tab_ref[8 + sh] * pltpu.roll(vk, sh, 0)
                    fz = rounded(grad * weight * gz)
                    value = value + tab_ref[16] * fz
                    for sh in range(1, 8):
                        value = value + tab_ref[16 + sh] * pltpu.roll(fz, sh, 0)
                    value = value + gm * weight * vk
                    out[x, k] = out[x, k] + value
        return carry

    velocity(0, 0)
    exchange_start(5, VV.at[0])
    velocity(1, 0)
    exchange_start(6, VV.at[1])

    exchange_end(0, W)
    for x in range(NX):
        for k in range(6):
            inv = jnp.where(sub_i < 6, DAMPING / jnp.where(sub_i < 6, W[x, k], 1.0), 0.0)
            INV[x, k] = inv
            V[x, k] = R[x, k] * inv
    apply_part(V, W)
    exchange_start(1, W)

    window_wait(0, csend, crecv)
    CF[...] = jnp.zeros(CF.shape, F32)
    for o in range(SPAN):
        for t in range(n_sub):
            packed = crecv[o, t]
            for ez in range(EZ):
                moved = pltpu.roll(packed, 128 - EY * ez, 1) if ez else packed
                moved = jnp.where(lane < EY, moved, 0.0)
                for q in range(4):
                    CF[EZ * o + ez + 1, q, EX * t : EX * t + EX, :] = moved[
                        EX * q : EX * q + EX, :
                    ]

    corners = [(a, c, d) for a in (0, 1) for c in (0, 1) for d in (0, 1)]

    def stencil(z, carry):
        shifted = {}
        for c in (0, 1):
            for q in range(4):
                base = CF[z + 1 - c, q]
                for a in (0, 1):
                    moved = pltpu.roll(base, 1, 0) if a else base
                    shifted[a, c, 0, q] = moved
                    shifted[a, c, 1, q] = pltpu.roll(moved, 1, 1)
        total = {}
        for ui, u in enumerate(corners):
            for vi, v in enumerate(corners):
                key = tuple(v[t] - u[t] for t in range(3))
                term = mac([(float(coarse[q][ui, vi]), shifted[u + (q,)]) for q in range(4)])
                total[key] = term if key not in total else total[key] + term
        for key, value in total.items():
            ST[z, 9 * (key[0] + 1) + 3 * (key[1] + 1) + key[2] + 1] = value
        diag = total[0, 0, 0]
        ST[z, 27] = jnp.where(diag > 0.0, 1.0 / jnp.where(diag > 0.0, diag, 1.0), 0.0)
        return carry

    lax.fori_loop(0, NZV // 2, stencil, 0)

    exchange_end(1, W)
    for x in range(NX):
        for k in range(6):
            V[x, k] = V[x, k] + (R[x, k] - W[x, k]) * INV[x, k]
    apply_part(V, W)

    one = jnp.ones((8, 128), F32)
    wz = jnp.where(sub_i < 5, one, 0.0)
    wz = jnp.where(jnp.logical_and(sub_i == 5, lane >= 128 - EY), 1.0, wz)
    low_half = jnp.where(has["zl"], 0.5, 1.0)
    high_half = jnp.where(has["zh"], 0.5, 1.0)
    wz = wz * jnp.where(jnp.logical_and(sub_i == 0, lane < EY), low_half, 1.0)
    wz = wz * jnp.where(jnp.logical_and(sub_i == 5, lane >= 128 - EY), high_half, 1.0)
    wend = wz * jnp.where(ey == EY - 1, 1.0, 0.0)
    xlow = jnp.where(has["xl"], 0.5, 1.0)
    xhigh = jnp.where(has["xh"], 0.5, 1.0)

    def unique(x, k):
        tile = wz if k < 5 else wend
        if x == 0:
            tile = tile * xlow
        if x == NX - 1:
            tile = tile * xhigh
        return tile

    acc = [[None, None] for _ in range(EX + 1)]
    for x in range(NX):
        rows = [unique(x, k) * R[x, k] - W[x, k] for k in range(6)]
        lines = [mac([(float(lin[k, d]), rows[k]) for k in range(6)]) for d in (0, 1)]
        ex = min(x // 5, EX - 1)
        i = x - 5 * ex
        for a in (0, 1):
            weight = float(lin[i, a])
            if weight == 0.0:
                continue
            for d in (0, 1):
                term = weight * lines[d]
                old = acc[ex + a][d]
                acc[ex + a][d] = term if old is None else old + term
    pieces = {}
    for c in (0, 1):
        for d in (0, 1):
            tile = jnp.zeros((8, 128), F32)
            for xv in range(EX + 1):
                row = jnp.sum(LJ[c] * acc[xv][d], axis=0, keepdims=True)
                tile = jnp.where(sub_i == xv, jnp.broadcast_to(row, (8, 128)), tile)
            pieces[c, d] = tile
    placed = [None] * (EZ + 1)
    for c in (0, 1):
        for ez in range(EZ):
            sums = None
            for d in (0, 1):
                tile = pieces[c, d]
                if ez:
                    tile = pltpu.roll(tile, 128 - EY * ez, 1)
                tile = jnp.where(lane < EY, tile, 0.0)
                if d:
                    tile = pltpu.roll(tile, 1, 1)
                sums = tile if sums is None else sums + tile
            old = placed[ez + c]
            placed[ez + c] = sums if old is None else old + sums
    message = placed[0]
    for zv in range(1, EZ + 1):
        rows_at, lanes_at = divmod(zv, 3)
        tile = placed[zv]
        if lanes_at:
            tile = pltpu.roll(tile, (EY + 8) * lanes_at, 1)
        if rows_at:
            tile = pltpu.roll(tile, (EX + 1) * rows_at, 0)
        message = message + tile
    rsend[...] = message
    rrecv[REACH, s] = message
    window_start(1, rsend, rrecv)
    lax.fori_loop(NZV // 2, NZV, stencil, 0)

    window_wait(1, rsend, rrecv)

    def window_sum(o, zv):
        rows_at, lanes_at = divmod(zv, 3)
        total = None
        for t in range(n_sub):
            tile = rrecv[o, t]
            if lanes_at:
                tile = pltpu.roll(tile, 128 - (EY + 8) * lanes_at, 1)
            here = jnp.logical_and(
                sub_i >= (EX + 1) * rows_at, sub_i < (EX + 1) * (rows_at + 1)
            )
            tile = jnp.where(jnp.logical_and(here, lane <= EY), tile, 0.0)
            if xs > 8:
                tile = jnp.concatenate([tile, jnp.zeros((xs - 8, 128), F32)], axis=0)
            shift = (EX * t - (EX + 1) * rows_at) % xs
            if shift:
                tile = pltpu.roll(tile, shift, 0)
            total = tile if total is None else total + tile
        return total

    center = (SPECTRUM_HIGH + SPECTRUM_LOW) / 2.0
    radius = (SPECTRUM_HIGH - SPECTRUM_LOW) / 2.0
    ratio = center / radius
    factor = 1.0 / ratio
    for z in range(NZV):
        o, zv = divmod(z, EZ)
        if o == SPAN:
            value = window_sum(o - 1, EZ)
        else:
            value = window_sum(o, zv)
            if zv == 0 and o > 0:
                value = value + window_sum(o - 1, EZ)
        CR[z] = value
        CU[0, z] = value * ST[z, 27] * (1.0 / center)
    first, last = REACH * EZ, REACH * EZ + EZ
    sol = [CU[0, z] for z in range(first, last + 1)]
    for sweep in range(CHEB_ITERS - 1):
        now, later = sweep % 2, (sweep + 1) % 2
        left = CHEB_ITERS - 2 - sweep
        nxt = 1.0 / (2.0 * ratio - factor)
        lo, hi = max(first - left, 0), min(last + left, NZV - 1)
        wide = {}
        for z in range(lo, hi + 1):
            for zz in (z - 1, z, z + 1):
                if zz in wide or not 0 <= zz < NZV:
                    continue
                base = CU[now, zz]
                sides = {}
                for dx in (-1, 0, 1):
                    mx = base if dx == 0 else pltpu.roll(base, (-dx) % xs, 0)
                    for dy in (-1, 0, 1):
                        sides[dx, dy] = mx if dy == 0 else pltpu.roll(mx, (-dy) % 128, 1)
                wide[zz] = sides
            total = None
            for dz in (-1, 0, 1):
                if not 0 <= z + dz < NZV:
                    continue
                for dx in (-1, 0, 1):
                    for dy in (-1, 0, 1):
                        term = ST[z, 9 * (dx + 1) + 3 * (dz + 1) + dy + 1] * wide[z + dz][dx, dy]
                        total = term if total is None else total + term
            residual = CR[z] - total
            CR[z] = residual
            fresh = (nxt * factor) * CU[now, z] + (2.0 * nxt / radius) * (residual * ST[z, 27])
            CU[later, z] = fresh
            if first <= z <= last:
                sol[z - first] = sol[z - first] + fresh
        factor = nxt

    own = []
    for zv in range(EZ + 1):
        tile = sol[zv]
        moved = tile
        for t in range(1, n_sub):
            moved = jnp.where(s == t, pltpu.roll(tile, (-EX * t) % xs, 0), moved)
        own.append(moved[0:8])
    corner_tiles = {}
    for c in (0, 1):
        for d in (0, 1):
            total = None
            for ez in range(EZ):
                tile = own[ez + c]
                if d:
                    tile = pltpu.roll(tile, 127, 1)
                tile = jnp.where(lane < EY, tile, 0.0)
                if ez:
                    tile = pltpu.roll(tile, EY * ez, 1)
                total = tile if total is None else total + tile
            corner_tiles[c, d] = total
    spread = []
    for xv in range(EX + 1):
        ends = []
        for d in (0, 1):
            ends.append(
                sum(
                    LJ[c] * jnp.broadcast_to(corner_tiles[c, d][xv : xv + 1, :], (8, 128))
                    for c in (0, 1)
                )
            )
        spread.append(
            [mac([(float(lin[k, d]), ends[d]) for d in (0, 1)]) for k in range(6)]
        )
    for x in range(NX):
        ex = min(x // 5, EX - 1)
        i = x - 5 * ex
        for k in range(6):
            V[x, k] = V[x, k] + mac([(float(lin[i, a]), spread[ex + a][k]) for a in (0, 1)])

    for idx in (2, 3):
        apply_part(V, W)
        exchange_start(idx, W)
        if idx == 2:
            velocity(2, 0)
            exchange_start(7, VV.at[2])
        else:
            for c in range(2):
                exchange_end(5 + c, VV.at[c])
                to_nodes(VV.at[c], velout_ref.at[c])
        exchange_end(idx, W)
        for x in range(NX):
            for k in range(6):
                V[x, k] = V[x, k] + (R[x, k] - W[x, k]) * INV[x, k]
    apply_part(V, W)
    num = jnp.zeros((8, 128), F32)
    den = jnp.zeros((8, 128), F32)
    for x in range(NX):
        for k in range(6):
            v = V[x, k]
            num = num + unique(x, k) * R[x, k] * v
            den = den + v * W[x, k]
    exchange_start(4, W)
    num_row = jnp.sum(num, axis=0, keepdims=True)
    den_row = jnp.sum(den, axis=0, keepdims=True)
    num_one = jnp.sum(num_row, axis=1, keepdims=True)
    den_one = jnp.sum(den_row, axis=1, keepdims=True)
    lane1 = lax.broadcasted_iota(jnp.int32, (1, 128), 1)
    psend[...] = jnp.where(lane1 < 64, num_one, den_one)

    def scatter(d, carry):
        pltpu.make_async_remote_copy(
            src_ref=psend,
            dst_ref=precv.at[d - 1],
            send_sem=p_sem.at[0],
            recv_sem=p_sem.at[1],
            device_id=device_of(lax.rem(me + d, n_dev)),
            device_id_type=MESH,
        ).start()
        return carry

    lax.fori_loop(1, n_dev, scatter, 0)
    to_nodes(V, pres_ref)
    exchange_end(7, VV.at[2])
    to_nodes(VV.at[2], velout_ref.at[2])
    exchange_end(4, W)
    to_nodes(W, res_ref)
    whole = pltpu.make_async_remote_copy(
        src_ref=precv,
        dst_ref=precv,
        send_sem=p_sem.at[0],
        recv_sem=p_sem.at[1],
        device_id=(b, s),
        device_id_type=MESH,
    )
    whole.wait_recv()
    both = psend[...] + jnp.sum(precv[...], axis=0)
    step = both[0:1, 0:1] / both[0:1, 64:65]
    for x in range(NX):
        pres_ref[x] = step * pres_ref[x]
        res_ref[x] = load_ref[x] - step * res_ref[x]
    whole.wait_send()
    for idx in range(EXCH):
        exchange_sent(idx)
    window_sent(0, csend, crecv)
    window_sent(1, rsend, rrecv)


def solution(mesh):
    n_blk, n_sub = mesh.shape["blk"], mesh.shape["sub"]
    n_dev = n_blk * n_sub
    xs = -(-(EX * n_sub + 2) // 8) * 8
    D, w, k1, lin, coarse = tables()
    Dh = bf16_round(D)
    tab = np.concatenate(
        [
            roll_tables(k1),
            roll_tables(Dh),
            roll_tables(Dh.T),
            col_tile(w),
            col_tile(lin[:, 0]),
            col_tile(lin[:, 1]),
            col_tile(np.diag(k1)),
        ]
    )
    pick, put = pick_matrices()

    def per_device(velocity, pressure_load, local_map, stiff_geo, mass_geo):
        vm = pl.BlockSpec(memory_space=pltpu.VMEM)
        field = (NX, 6, 8, 128)
        out = pl.pallas_call(
            functools.partial(kernel, n_blk, n_sub, xs),
            out_shape=(
                jax.ShapeDtypeStruct((3, NX, NZ, NY), F32),
                jax.ShapeDtypeStruct((NX, NZ, NY), F32),
                jax.ShapeDtypeStruct((NX, NZ, NY), F32),
            ),
            in_specs=[vm, vm, pl.BlockSpec(memory_space=pl.ANY)] + [vm] * 5,
            out_specs=(vm, vm, vm),
            scratch_shapes=[
                pltpu.VMEM(field, F32),
                pltpu.VMEM(field, F32),
                pltpu.VMEM((NX, NZP, NYP), F32),
                pltpu.VMEM((8, EX * EZ * EY), jnp.int32),
                pltpu.VMEM(field, F32),
                pltpu.VMEM(field, F32),
                pltpu.VMEM((3,) + field, F32),
                pltpu.VMEM(field, F32),
                pltpu.VMEM((EX, 8, 128), F32),
                pltpu.VMEM((3, NX, 8, 128), F32),
                pltpu.VMEM((4, EX, 8, 128), F32),
                pltpu.VMEM((EXCH, 2, 6, 8, 128), F32),
                pltpu.VMEM((EXCH, 2, 6, 8, 128), F32),
                pltpu.VMEM((EXCH, 2, ZT, 8, 128), F32),
                pltpu.VMEM((EXCH, 2, ZT, 8, 128), F32),
                pltpu.VMEM((EXCH, 2, 2, 8, 128), F32),
                pltpu.VMEM((8, 128), F32),
                pltpu.VMEM((SPAN, n_sub, 8, 128), F32),
                pltpu.VMEM((8, 128), F32),
                pltpu.VMEM((SPAN, n_sub, 8, 128), F32),
                pltpu.VMEM((NZV + 1, 4, xs, 128), F32),
                pltpu.VMEM((NZV, 28, xs, 128), F32),
                pltpu.VMEM((2, NZV, xs, 128), F32),
                pltpu.VMEM((NZV, xs, 128), F32),
                pltpu.VMEM((1, 128), F32),
                pltpu.VMEM((n_dev - 1, 1, 128), F32),
                pltpu.SemaphoreType.DMA((EXCH, 8)),
                pltpu.SemaphoreType.DMA((EXCH, 8)),
                pltpu.SemaphoreType.DMA((2, SPAN, n_sub)),
                pltpu.SemaphoreType.DMA((2, SPAN, n_sub)),
                pltpu.SemaphoreType.DMA((2,)),
                pltpu.SemaphoreType.DMA,
            ],
            compiler_params=pltpu.CompilerParams(
                collective_id=0, has_side_effects=True, vmem_limit_bytes=60 << 20
            ),
        )(
            velocity.reshape(3, NX, NZ, NY),
            pressure_load.reshape(NX, NZ, NY),
            local_map,
            stiff_geo,
            mass_geo.reshape(1, mass_geo.shape[0]),
            jnp.asarray(tab, F32),
            jnp.asarray(pick, BF16),
            jnp.asarray(put, BF16),
        )
        return (out[0].reshape(3, NLOC), out[1].reshape(NLOC), out[2].reshape(NLOC))

    in_specs = (
        P(None, ("blk", "sub")),
        P(("blk", "sub")),
        P(None, ("blk", "sub")),
        P(None, ("blk", "sub")),
        P(("blk", "sub")),
    )
    out_specs = (P(None, ("blk", "sub")), P(("blk", "sub")), P(("blk", "sub")))
    return jax.shard_map(
        per_device, mesh=mesh, in_specs=in_specs, out_specs=out_specs, check_vma=False
    )
```

profile of v0, /device:TPU:0, one launch (start us, length us, event | category | flops | bytes accessed | tf_op | source)
XLA Modules:
  0.0 47.9 jit_solution(15121069769024767929)
XLA Ops:
  0.6 2.0 %reshape.25.load_ref = f32[11,21,161]{2,1,0:T(8,128)} reshape(f32[37191]{0:T(1024)} %param.9) | data formatting | bytes 297528 | tf_op jit(solution)/shard_map/reshape | solution.py:905
  2.6 2.7 %reshape.24.vel_ref = f32[3,11,21,161]{3,2,1,0:T(8,128)} reshape(f32[3,37191]{1,0:T(4,128)} %param.8) | data formatting | bytes 892584 | tf_op jit(solution)/shard_map/reshape | solution.py:904
  5.3 38.0 %shard_map.103 = (f32[3,11,21,161]{3,2,1,0:T(8,128)}, f32[11,21,161]{2,1,0:T(8,128)}, f32[11,21,161]{2,1,0:T(8,128)}) custom-call(f32[3,11,21,161]{3,2,1,0:T(8,128)} %reshape.24.vel_ref, f32[11,21,161]{2,1,0:T(8,128)} %reshape.25.load_ref, s32[216,256]{1,0:T(8,128)} %map_hbm.1, f32[3,256]{1,0:T(4,128)} %stiff_ref.1, f32[1,256]{1,0:T(1,128)} %bitcast.1, ...), custom_call_target="tpu_custom_call" | custom-call | tf_op jit(solution)/shard_map/pallas_call | solution.py:857
  43.3 0.0 copy-start.1
  43.3 2.6 %reshape.27 = f32[3,37191]{1,0:T(4,128)} reshape(f32[3,11,21,161]{3,2,1,0:T(8,128)} %get-tuple-element.6) | data formatting | bytes 892584 | tf_op jit(solution)/shard_map/reshape | solution.py:913
  45.9 0.0 copy-done.1
  45.9 0.0 copy-start
  45.9 1.0 %reshape.28 = f32[37191]{0:T(1024)} reshape(f32[11,21,161]{2,1,0:T(8,128)S(1)} %copy-done.1) | data formatting | bytes 297528 | tf_op jit(solution)/shard_map/reshape | solution.py:913
  46.9 0.0 copy-done
  46.9 1.0 %reshape.29 = f32[37191]{0:T(1024)} reshape(f32[11,21,161]{2,1,0:T(8,128)S(1)} %copy-done) | data formatting | bytes 297528 | tf_op jit(solution)/shard_map/reshape | solution.py:913
Async XLA Ops:
  43.3 2.6 %copy-start.1 = (f32[11,21,161]{2,1,0:T(8,128)S(1)}, f32[11,21,161]{2,1,0:T(8,128)}, u32[]{:S(2)}) copy-start(f32[11,21,161]{2,1,0:T(8,128)} %get-tuple-element.7) | copy-start | bytes 446296
  45.9 1.0 %copy-start = (f32[11,21,161]{2,1,0:T(8,128)S(1)}, f32[11,21,161]{2,1,0:T(8,128)}, u32[]{:S(2)}) copy-start(f32[11,21,161]{2,1,0:T(8,128)} %get-tuple-element.8) | copy-start | bytes 446296
where the time goes:
time: 48.2 us; the launch traced here: 47.9 us
  Pallas kernels  38 us (79%)
  local copies, waits for them, and re-layouts  9.26 us (19%)
  between operations  0.65 us (1%)
    pallas_call x1, Pallas kernels, per_device(): pl.pallas_call(functools.partial(kernel, n_blk, n_sub, xs), out_shape=(ja...  38 us
    reshape x3, local copies, waits for them, and re-layouts, per_device(): return (out[0].reshape(3, NLOC), out[1].reshape(NLOC), out[2].reshape(NLOC))  4.61 us
    reshape x1, local copies, waits for them, and re-layouts, per_device(): velocity.reshape(3, NX, NZ, NY)  2.69 us
    reshape x1, local copies, waits for them, and re-layouts, per_device(): pressure_load.reshape(NX, NZ, NY)  1.95 us

commit v1 on v0

--- a/solution.py
+++ b/solution.py
@@ -19,10 +19,16 @@
 NLOC = NX * NZ * NY
 NZP = 24
 NYP = 256
-REACH = -(-(CHEB_ITERS - 1) // EZ)
+HALO = 2
+DEPTH = CHEB_ITERS - 1 + HALO
+REACH = -(-DEPTH // EZ)
 SPAN = 2 * REACH + 1
 NZV = SPAN * EZ + 1
-EXCH = 8
+FIRST = REACH * EZ
+LAST_V = FIRST + EZ
+ZLO = FIRST - DEPTH
+ZHI = LAST_V + DEPTH
+EXCH = 7
 ZT = -(-NX // 4)
 LAST = (NX - 1) % 4
 
@@ -108,17 +114,24 @@
     n_blk,
     n_sub,
     xs,
+    vel_hbm,
+    load_hbm,
+    map_hbm,
+    stiff_hbm,
+    mass_hbm,
+    tab_hbm,
+    pick_hbm,
+    put_hbm,
+    velout_ref,
+    pres_ref,
+    res_ref,
     vel_ref,
     load_ref,
-    map_hbm,
     stiff_ref,
     mass_ref,
     tab_ref,
     pick_ref,
     put_ref,
-    velout_ref,
-    pres_ref,
-    res_ref,
     V,
     W,
     FS,
@@ -129,6 +142,7 @@
     VE,
     GX,
     GC,
+    GE,
     SG,
     xsend,
     xrecv,
@@ -139,6 +153,8 @@
     crecv,
     rsend,
     rrecv,
+    bsend,
+    brecv,
     CF,
     ST,
     CU,
@@ -149,8 +165,10 @@
     ex_recv,
     c_send,
     c_recv,
+    h_send,
+    h_recv,
     p_sem,
-    m_sem,
+    in_sem,
 ):
     D, w, k1, lin, coarse = tables()
     Dh = bf16_round(D)
@@ -162,6 +180,32 @@
     def device_of(linear):
         return (linear // n_sub, lax.rem(linear, n_sub))
 
+    barrier = pltpu.get_barrier_semaphore()
+
+    def greet(d, carry):
+        pl.semaphore_signal(
+            barrier, inc=1, device_id=device_of(lax.rem(me + d, n_dev)), device_id_type=MESH
+        )
+        return carry
+
+    lax.fori_loop(1, n_dev, greet, 0)
+
+    fetch = {}
+    for at, (name, src, dst) in enumerate(
+        (
+            ("map", map_hbm.at[0:8, :], map_ref),
+            ("stiff", stiff_hbm, stiff_ref),
+            ("mass", mass_hbm, mass_ref),
+            ("tab", tab_hbm, tab_ref),
+            ("load", load_hbm, load_ref),
+            ("pick", pick_hbm, pick_ref),
+            ("vel", vel_hbm, vel_ref),
+            ("put", put_hbm, put_ref),
+        )
+    ):
+        fetch[name] = pltpu.make_async_copy(src, dst, in_sem.at[at])
+        fetch[name].start()
+
     has = {
         "xl": s > 0,
         "xh": s < n_sub - 1,
@@ -183,6 +227,7 @@
         @pl.when(jnp.logical_not(has[name]))
         def _(side=side):
             zero(zrecv.at[:, side])
+            zero(brecv.at[:, side])
 
     for zs, zname in ((0, "zl"), (1, "zh")):
         for xside, xname in ((0, "xl"), (1, "xh")):
@@ -199,27 +244,21 @@
             zero(crecv.at[o])
             zero(rrecv.at[o])
 
-    barrier = pltpu.get_barrier_semaphore()
-    map_copy = pltpu.make_async_copy(map_hbm.at[0:8, :], map_ref, m_sem)
-    map_copy.start()
-
-    def greet(d, carry):
-        pl.semaphore_signal(
-            barrier, inc=1, device_id=device_of(lax.rem(me + d, n_dev)), device_id_type=MESH
-        )
-        return carry
-
-    lax.fori_loop(1, n_dev, greet, 0)
+    CF[...] = jnp.zeros(CF.shape, F32)
+    FS[...] = jnp.zeros(FS.shape, F32)
 
     lane = lax.broadcasted_iota(jnp.int32, (8, 128), 1)
     sub_i = lax.broadcasted_iota(jnp.int32, (8, 128), 0)
     lane88 = lax.broadcasted_iota(jnp.int32, (8 * NX, 768), 1) // EY % EZ
     row88 = lax.broadcasted_iota(jnp.int32, (8 * NX, 768), 0) % 8
+    ey = lane % EY
+    lane6 = lax.broadcasted_iota(jnp.int32, (6, 128), 1)
+    group6 = lane6 // EY
+    group = lane // EY
     CT = lambda q: tab_ref[q]
-    WJ = tab_ref[24]
-    LJ = (tab_ref[25], tab_ref[26])
-
-    FS[...] = jnp.zeros(FS.shape, F32)
+
+    def moved(tile, shift):
+        return tile if shift % 128 == 0 else pltpu.roll(tile, shift % 128, 1)
 
     def to_elements(field, dest, exact):
         FS[:, 0:NZ, 0:NY] = field[...]
@@ -253,7 +292,10 @@
             piece = got[8 * NX * ez : 8 * NX * (ez + 1)].reshape(NX, 8, NYP)
             dest[:, 5 * ez : 5 * ez + 6, :] = piece[:, :6, :NY]
 
-    map_copy.wait()
+    for name in ("map", "stiff", "mass", "tab"):
+        fetch[name].wait()
+    WJ = tab_ref[24]
+    LJ = (tab_ref[25], tab_ref[26])
     corner = map_ref[0:1, :]
     slot = (corner // (NZ * NY) // 5 * EZ + corner // NY % NZ // 5) * EY + corner % NY // 5
     count = EX * EZ * EY
@@ -272,42 +314,67 @@
         pack, hot.astype(BF16), (((1,), (1,)), ((), ())), preferred_element_type=F32
     )
     sorted_geo = got[0:8] + got[8:16] + got[16:24]
-    g = [
-        [
-            jnp.broadcast_to(sorted_geo[q : q + 1, 128 * ex : 128 * ex + 128], (8, 128))
-            for ex in range(EX)
-        ]
-        for q in range(4)
-    ]
-    for q in range(4):
-        for ex in range(EX):
-            SG[q, ex] = g[q][ex]
-    for ex in range(EX):
-        GX[ex] = WJ * g[0][ex]
-    for x in range(NX):
-        share = [(ex, x - 5 * ex) for ex in range(EX) if 0 <= x - 5 * ex <= 5]
-        GC[0, x] = WJ * mac([(float(w[i]), g[2][ex]) for ex, i in share])
-        GC[1, x] = mac([(float(w[i]), g[1][ex]) for ex, i in share])
-        GC[2, x] = WJ * mac([(float(MASS_SHARE * w[i]), g[3][ex]) for ex, i in share])
     stack = jnp.zeros((8, 128), F32)
     for q in range(4):
         for ex in range(EX):
-            stack = jnp.where(sub_i == EX * q + ex, g[q][ex], stack)
+            row = jnp.broadcast_to(
+                sorted_geo[q : q + 1, 128 * ex : 128 * ex + 128], (8, 128)
+            )
+            SG[q, ex] = row
+            stack = jnp.where(sub_i == EX * q + ex, row, stack)
     csend[...] = stack
 
-    def diagonal_part():
+    def geometry(h, tile):
+        g = [
+            [
+                jnp.broadcast_to(tile[EX * q + ex : EX * q + ex + 1, :], (8, 128))
+                for ex in range(EX)
+            ]
+            for q in range(4)
+        ]
+        for ex in range(EX):
+            GX[h, 1 + ex] = WJ * g[0][ex]
+        for x in range(NX):
+            share = [(ex, x - 5 * ex) for ex in range(EX) if 0 <= x - 5 * ex <= 5]
+            GC[h, 0, x] = WJ * mac([(float(w[i]), g[2][ex]) for ex, i in share])
+            GC[h, 1, x] = mac([(float(w[i]), g[1][ex]) for ex, i in share])
+            GC[h, 2, x] = WJ * mac([(float(MASS_SHARE * w[i]), g[3][ex]) for ex, i in share])
+
+    def face_geometry(h, tiles):
+        for face, (tile, ex) in enumerate(zip(tiles, (EX - 1, 0))):
+            g = [
+                jnp.broadcast_to(tile[EX * q + ex : EX * q + ex + 1, :], (8, 128))
+                for q in range(4)
+            ]
+            x = (NX - 1) * face
+            GX[h, (EX + 1) * face] = WJ * g[0]
+            GE[h, face, 0] = GC[h, 0, x] + WJ * (float(w[0]) * g[2])
+            GE[h, face, 1] = GC[h, 1, x] + float(w[0]) * g[1]
+            GE[h, face, 2] = GC[h, 2, x] + WJ * (float(MASS_SHARE * w[0]) * g[3])
+
+    def whole_geometry(h, x):
+        if x == 0:
+            return tuple(GE[h, 0, q] for q in range(3))
+        if x == NX - 1:
+            return tuple(GE[h, 1, q] for q in range(3))
+        return tuple(GC[h, q, x] for q in range(3))
+
+    def diagonal_part(h):
         kj = tab_ref[27]
         for x in range(NX):
-            share = [(ex, x - 5 * ex) for ex in range(EX) if 0 <= x - 5 * ex <= 5]
-            gx = mac([(float(k1[i, i]), GX[ex]) for ex, i in share])
-            gy, gz, gm = GC[0, x], GC[1, x], GC[2, x]
+            share = [
+                (ex, x - 5 * ex) for ex in range(-1, EX + 1) if 0 <= x - 5 * ex <= 5
+            ]
+            gx = mac([(float(k1[i, i]), GX[h, 1 + ex]) for ex, i in share])
+            gy, gz, gm = whole_geometry(h, x)
             base = gx + gz * kj + gm
             for k in range(6):
-                W[x, k] = float(w[k]) * base + float(k1[k, k]) * gy
-
-    def apply_part(src, dst):
+                W[h, x, k] = float(w[k]) * base + float(k1[k, k]) * gy
+
+    def apply_part(h):
+        src, dst = V.at[h], W.at[h]
         for ex in range(EX):
-            gx = GX[ex]
+            gx = GX[h, 1 + ex]
             for k in range(6):
                 vs = [src[5 * ex + m, k] for m in range(6)]
                 gk = float(w[k]) * gx
@@ -317,7 +384,7 @@
                         value = value + dst[5 * ex, k]
                     dst[5 * ex + i, k] = value
         for x in range(NX):
-            gy, gz, gm = GC[0, x], GC[1, x], GC[2, x]
+            gy, gz, gm = GC[h, 0, x], GC[h, 1, x], GC[h, 2, x]
             vs = [src[x, m] for m in range(6)]
             for k in range(6):
                 vk = vs[k]
@@ -328,11 +395,30 @@
                 value = value + gy * mac([(float(k1[k, m]), vs[m]) for m in range(6)])
                 dst[x, k] = dst[x, k] + value
 
-    ey = lane % EY
-    lane6 = lax.broadcasted_iota(jnp.int32, (6, 128), 1)
+    def fold_y(F):
+        for x in range(NX):
+            low, high = F[x, 0], F[x, 5]
+            F[x, 0] = low + jnp.where(ey > 0, pltpu.roll(high, 1, 1), 0.0)
+            F[x, 5] = high + jnp.where(ey < EY - 1, pltpu.roll(low, 127, 1), 0.0)
+
+    def fold_z(F, both):
+        for x in range(NX):
+            z0, z5 = F[0, x, :, 0, :], F[0, x, :, 5, :]
+            h0, h5 = F[1, x, :, 0, :], F[1, x, :, 5, :]
+            z0_up, z5_up = pltpu.roll(z0, EY, 1), pltpu.roll(z5, EY, 1)
+            z0_down, z5_down = pltpu.roll(z0, 128 - EY, 1), pltpu.roll(z5, 128 - EY, 1)
+            h0_up, h5_up = pltpu.roll(h0, EY, 1), pltpu.roll(h5, EY, 1)
+            h0_down, h5_down = pltpu.roll(h0, 128 - EY, 1), pltpu.roll(h5, 128 - EY, 1)
+            F[0, x, :, 0, :] = z0 + jnp.where(lane6 < EY, h5_down, z5_up)
+            F[0, x, :, 5, :] = z5 + jnp.where(lane6 >= 128 - EY, h0_up, z0_down)
+            if both:
+                add0 = jnp.where(group6 == 2, z5_down, h5_up)
+                add5 = jnp.where(group6 == 1, z0_up, h0_down)
+                F[1, x, :, 0, :] = h0 + jnp.where(group6 == 0, 0.0, add0)
+                F[1, x, :, 5, :] = h5 + jnp.where(group6 == 3, 0.0, add5)
 
     def link(idx, slot_no, src, dst, device):
-        return pltpu.make_async_remote_copy(
+        return lambda: pltpu.make_async_remote_copy(
             src_ref=src,
             dst_ref=dst,
             send_sem=ex_send.at[idx, slot_no],
@@ -341,11 +427,15 @@
             device_id_type=MESH,
         )
 
-    def links(idx):
+    def x_links(idx):
+        return [
+            (has["xl"], has["xh"], link(idx, 1, xsend.at[idx, 0], xrecv.at[idx, 1], (b, s - 1))),
+            (has["xh"], has["xl"], link(idx, 0, xsend.at[idx, 1], xrecv.at[idx, 0], (b, s + 1))),
+        ]
+
+    def z_links(idx):
         both = jnp.logical_and
         out = [
-            (has["xl"], has["xh"], link(idx, 1, xsend.at[idx, 0], xrecv.at[idx, 1], (b, s - 1))),
-            (has["xh"], has["xl"], link(idx, 0, xsend.at[idx, 1], xrecv.at[idx, 0], (b, s + 1))),
             (has["zl"], has["zh"], link(idx, 3, zsend.at[idx, 0], zrecv.at[idx, 1], (b - 1, s))),
             (has["zh"], has["zl"], link(idx, 2, zsend.at[idx, 1], zrecv.at[idx, 0], (b + 1, s))),
         ]
@@ -366,51 +456,80 @@
                 )
         return out
 
-    def exchange_start(idx, F):
-        for x in range(NX):
-            low, high = F[x, 0], F[x, 5]
-            F[x, 0] = low + jnp.where(ey > 0, pltpu.roll(high, 1, 1), 0.0)
-            F[x, 5] = high + jnp.where(ey < EY - 1, pltpu.roll(low, 127, 1), 0.0)
+    def halo_links(idx):
+        def one(side, device):
+            return lambda: pltpu.make_async_remote_copy(
+                src_ref=bsend.at[idx, side],
+                dst_ref=brecv.at[idx, 1 - side],
+                send_sem=h_send.at[idx, side],
+                recv_sem=h_recv.at[idx, 1 - side],
+                device_id=device,
+                device_id_type=MESH,
+            )
+
+        return [
+            (has["zl"], has["zh"], one(0, (b - 1, s))),
+            (has["zh"], has["zl"], one(1, (b + 1, s))),
+        ]
+
+    def links_start(links):
+        for there, _, copy in links:
+
+            @pl.when(there)
+            def _(copy=copy):
+                copy().start()
+
+    def links_wait(links):
+        for _, here, copy in links:
+
+            @pl.when(here)
+            def _(copy=copy):
+                copy().wait_recv()
+
+    def links_sent(links):
+        for there, _, copy in links:
+
+            @pl.when(there)
+            def _(copy=copy):
+                copy().wait_send()
+
+    def x_start(idx, F):
         xsend[idx, 0] = F[0]
         xsend[idx, 1] = F[NX - 1]
-        group = lane6 // EY
+        links_start(x_links(idx))
+
+    def x_end(idx, F):
+        links_wait(x_links(idx))
+        F[0] = F[0] + xrecv[idx, 0]
+        F[NX - 1] = F[NX - 1] + xrecv[idx, 1]
+
+    def exchange_start(idx, F):
+        fold_y(F)
+        x_start(idx, F)
         for t in range(ZT):
             low = high = jnp.zeros((6, 128), F32)
             for m in range(4):
                 x = 4 * t + m
                 if x >= NX:
                     continue
-                z0, z5 = F[x, :, 0, :], F[x, :, 5, :]
-                if m:
-                    z0 = pltpu.roll(z0, EY * m, 1)
-                if m < 3:
-                    z5 = pltpu.roll(z5, EY * (m + 1), 1)
-                low = jnp.where(group == m, z0, low)
-                high = jnp.where(group == m, z5, high)
+                low = jnp.where(group6 == m, moved(F[x, :, 0, :], EY * m), low)
+                high = jnp.where(group6 == m, moved(F[x, :, 5, :], EY * (m + 1)), high)
             zsend[idx, 0, t, 0:6, :] = low
             zsend[idx, 1, t, 0:6, :] = high
-        for there, _, copy in links(idx):
-
-            @pl.when(there)
-            def _(copy=copy):
-                copy.start()
-
-    def exchange_end(idx, F):
-        for _, here, copy in links(idx):
-
-            @pl.when(here)
-            def _(copy=copy):
-                copy.wait_recv()
-
-        F[0] = F[0] + xrecv[idx, 0]
-        F[NX - 1] = F[NX - 1] + xrecv[idx, 1]
+        links_start(z_links(idx))
+
+    def inner_z(F):
         for x in range(NX):
             z0, z5 = F[x, :, 0, :], F[x, :, 5, :]
+            F[x, :, 0, :] = z0 + jnp.where(lane6 < EY, 0.0, pltpu.roll(z5, EY, 1))
+            F[x, :, 5, :] = z5 + jnp.where(
+                lane6 >= 128 - EY, 0.0, pltpu.roll(z0, 128 - EY, 1)
+            )
+
+    def outer_z(idx, F):
+        links_wait(z_links(idx))
+        for x in range(NX):
             t, m = divmod(x, 4)
-
-            def moved(tile, shift):
-                return tile if shift % 128 == 0 else pltpu.roll(tile, shift % 128, 1)
-
             near = moved(zrecv[idx, 0, t, 0:6, :], -EY * m)
             far = moved(zrecv[idx, 1, t, 0:6, :], 128 - EY - EY * m)
             if x == 0:
@@ -419,15 +538,35 @@
             if x == NX - 1:
                 near = near + drecv[idx, 0, 1, 0:6, :]
                 far = far + moved(drecv[idx, 1, 1, 0:6, :], 128 - EY)
-            F[x, :, 0, :] = z0 + jnp.where(lane6 < EY, near, pltpu.roll(z5, EY, 1))
-            F[x, :, 5, :] = z5 + jnp.where(lane6 >= 128 - EY, far, pltpu.roll(z0, 128 - EY, 1))
-
-    def exchange_sent(idx):
-        for there, _, copy in links(idx):
-
-            @pl.when(there)
-            def _(copy=copy):
-                copy.wait_send()
+            F[x, :, 0, :] = F[x, :, 0, :] + jnp.where(lane6 < EY, near, 0.0)
+            F[x, :, 5, :] = F[x, :, 5, :] + jnp.where(lane6 >= 128 - EY, far, 0.0)
+
+    def exchange_end(idx, F):
+        x_end(idx, F)
+        inner_z(F)
+        outer_z(idx, F)
+
+    def halo_start(idx, src):
+        for t in range(ZT):
+            for k in range(6):
+                low = high = jnp.zeros((8, 128), F32)
+                for m in range(4):
+                    x = 4 * t + m
+                    if x >= NX:
+                        continue
+                    tile = src(x, k)
+                    low = jnp.where(group == m, moved(tile, EY * m), low)
+                    high = jnp.where(group == m, moved(tile, EY * (m + 1)), high)
+                bsend[idx, 0, t, k] = low
+                bsend[idx, 1, t, k] = high
+
+    def halo_unpack(idx, dst):
+        for x in range(NX):
+            t, m = divmod(x, 4)
+            for k in range(6):
+                low = moved(brecv[idx, 0, t, k], EY - EY * m)
+                high = moved(brecv[idx, 1, t, k], 2 * EY - EY * m)
+                dst[x, k] = jnp.where(group == 1, low, jnp.where(group == 2, high, 0.0))
 
     def window_copies(which, src, dst):
         out = []
@@ -438,22 +577,27 @@
                 peer_s = lax.rem(s + ds, n_sub)
                 target = b + off
                 sending = jnp.logical_and(target >= 0, target < n_blk)
-                copy = pltpu.make_async_remote_copy(
-                    src_ref=src,
-                    dst_ref=dst.at[REACH - off, s],
-                    send_sem=c_send.at[which, REACH + off, ds],
-                    recv_sem=c_recv.at[which, REACH - off, s],
-                    device_id=(target, peer_s),
-                    device_id_type=MESH,
-                )
-                arrive = pltpu.make_async_remote_copy(
-                    src_ref=src,
-                    dst_ref=dst.at[REACH + off, peer_s],
-                    send_sem=c_send.at[which, REACH + off, ds],
-                    recv_sem=c_recv.at[which, REACH + off, peer_s],
-                    device_id=(target, peer_s),
-                    device_id_type=MESH,
-                )
+
+                def copy(off=off, ds=ds, peer_s=peer_s, target=target):
+                    return pltpu.make_async_remote_copy(
+                        src_ref=src,
+                        dst_ref=dst.at[REACH - off, s],
+                        send_sem=c_send.at[which, REACH + off, ds],
+                        recv_sem=c_recv.at[which, REACH - off, s],
+                        device_id=(target, peer_s),
+                        device_id_type=MESH,
+                    )
+
+                def arrive(off=off, ds=ds, peer_s=peer_s, target=target):
+                    return pltpu.make_async_remote_copy(
+                        src_ref=src,
+                        dst_ref=dst.at[REACH + off, peer_s],
+                        send_sem=c_send.at[which, REACH + off, ds],
+                        recv_sem=c_recv.at[which, REACH + off, peer_s],
+                        device_id=(target, peer_s),
+                        device_id_type=MESH,
+                    )
+
                 out.append((sending, copy, arrive))
         return out
 
@@ -462,32 +606,23 @@
 
             @pl.when(sending)
             def _(copy=copy):
-                copy.start()
+                copy().start()
 
     def window_wait(which, src, dst):
         for sending, _, arrive in window_copies(which, src, dst):
 
             @pl.when(sending)
             def _(arrive=arrive):
-                arrive.wait_recv()
+                arrive().wait_recv()
 
     def window_sent(which, src, dst):
         for sending, copy, _ in window_copies(which, src, dst):
 
             @pl.when(sending)
             def _(copy=copy):
-                copy.wait_send()
-
-    diagonal_part()
-    to_elements(load_ref, R, True)
-    crecv[REACH, s] = csend[...]
-
-    pl.semaphore_wait(barrier, n_dev - 1)
-
-    exchange_start(0, W)
-    window_start(0, csend, crecv)
-
-    def velocity(c, carry):
+                copy().wait_send()
+
+    def velocity(c):
         to_elements(vel_ref.at[c], VE, False)
         out = VV.at[c]
         rounded = lambda value: value.astype(BF16).astype(F32)
@@ -526,32 +661,59 @@
                         value = value + tab_ref[16 + sh] * pltpu.roll(fz, sh, 0)
                     value = value + gm * weight * vk
                     out[x, k] = out[x, k] + value
+
+    geometry(0, stack)
+    fetch["load"].wait()
+    fetch["pick"].wait()
+    to_elements(load_ref, R.at[0], True)
+    halo_start(0, lambda x, k: R[0, x, k])
+    crecv[REACH, s] = stack
+    fetch["vel"].wait()
+
+    pl.semaphore_wait(barrier, n_dev - 1)
+
+    window_start(0, csend, crecv)
+    links_start(halo_links(0))
+    def component(c, carry):
+        velocity(c)
+        exchange_start(c, VV.at[c])
         return carry
 
-    velocity(0, 0)
-    exchange_start(5, VV.at[0])
-    velocity(1, 0)
-    exchange_start(6, VV.at[1])
-
-    exchange_end(0, W)
-    for x in range(NX):
-        for k in range(6):
-            inv = jnp.where(sub_i < 6, DAMPING / jnp.where(sub_i < 6, W[x, k], 1.0), 0.0)
-            INV[x, k] = inv
-            V[x, k] = R[x, k] * inv
-    apply_part(V, W)
-    exchange_start(1, W)
+    lax.fori_loop(0, 3, component, 0)
 
     window_wait(0, csend, crecv)
-    CF[...] = jnp.zeros(CF.shape, F32)
+
+    def beside(t):
+        low, high = crecv[REACH - 1, t], crecv[REACH + 1, t]
+        return jnp.where(lane < 2 * EY, pltpu.roll(low, 64, 1), pltpu.roll(high, 64, 1))
+
+    left_s, right_s = jnp.maximum(s - 1, 0), jnp.minimum(s + 1, n_sub - 1)
+    left_on = jnp.where(has["xl"], 1.0, 0.0)
+    right_on = jnp.where(has["xh"], 1.0, 0.0)
+    geometry(1, beside(s))
+    face_geometry(0, (crecv[REACH, left_s] * left_on, crecv[REACH, right_s] * right_on))
+    face_geometry(1, (beside(left_s) * left_on, beside(right_s) * right_on))
+    for h in range(2):
+        diagonal_part(h)
+    fold_z(W, True)
+    for h in range(2):
+        fold_y(W.at[h])
+    for h in range(2):
+        for x in range(NX):
+            for k in range(6):
+                full = W[h, x, k]
+                good = full > 0.0
+                INV[h, x, k] = jnp.where(good, DAMPING / jnp.where(good, full, 1.0), 0.0)
+
     for o in range(SPAN):
         for t in range(n_sub):
             packed = crecv[o, t]
             for ez in range(EZ):
-                moved = pltpu.roll(packed, 128 - EY * ez, 1) if ez else packed
-                moved = jnp.where(lane < EY, moved, 0.0)
+                if not ZLO - 1 <= EZ * o + ez <= ZHI:
+                    continue
+                tile = jnp.where(lane < EY, moved(packed, -EY * ez), 0.0)
                 for q in range(4):
-                    CF[EZ * o + ez + 1, q, EX * t : EX * t + EX, :] = moved[
+                    CF[EZ * o + ez + 1, q, EX * t : EX * t + EX, :] = tile[
                         EX * q : EX * q + EX, :
                     ]
 
@@ -563,9 +725,9 @@
             for q in range(4):
                 base = CF[z + 1 - c, q]
                 for a in (0, 1):
-                    moved = pltpu.roll(base, 1, 0) if a else base
-                    shifted[a, c, 0, q] = moved
-                    shifted[a, c, 1, q] = pltpu.roll(moved, 1, 1)
+                    up = pltpu.roll(base, 1, 0) if a else base
+                    shifted[a, c, 0, q] = up
+                    shifted[a, c, 1, q] = pltpu.roll(up, 1, 1)
         total = {}
         for ui, u in enumerate(corners):
             for vi, v in enumerate(corners):
@@ -578,13 +740,25 @@
         ST[z, 27] = jnp.where(diag > 0.0, 1.0 / jnp.where(diag > 0.0, diag, 1.0), 0.0)
         return carry
 
-    lax.fori_loop(0, NZV // 2, stencil, 0)
-
-    exchange_end(1, W)
+    cut_a = ZLO + (ZHI + 1 - ZLO) // 3
+    cut_b = ZLO + (ZHI + 1 - ZLO) * 2 // 3
+    lax.fori_loop(ZLO, cut_a, stencil, 0)
+
+    links_wait(halo_links(0))
+    halo_unpack(0, R.at[1])
+    for h in range(2):
+        for x in range(NX):
+            for k in range(6):
+                V[h, x, k] = R[h, x, k] * INV[h, x, k]
+        apply_part(h)
+    fold_z(W, False)
+    fold_y(W.at[0])
+    x_start(5, W.at[0])
+    x_end(5, W.at[0])
     for x in range(NX):
         for k in range(6):
-            V[x, k] = V[x, k] + (R[x, k] - W[x, k]) * INV[x, k]
-    apply_part(V, W)
+            V[0, x, k] = V[0, x, k] + (R[0, x, k] - W[0, x, k]) * INV[0, x, k]
+    apply_part(0)
 
     one = jnp.ones((8, 128), F32)
     wz = jnp.where(sub_i < 5, one, 0.0)
@@ -607,7 +781,7 @@
 
     acc = [[None, None] for _ in range(EX + 1)]
     for x in range(NX):
-        rows = [unique(x, k) * R[x, k] - W[x, k] for k in range(6)]
+        rows = [unique(x, k) * R[0, x, k] - W[0, x, k] for k in range(6)]
         lines = [mac([(float(lin[k, d]), rows[k]) for k in range(6)]) for d in (0, 1)]
         ex = min(x // 5, EX - 1)
         i = x - 5 * ex
@@ -632,10 +806,7 @@
         for ez in range(EZ):
             sums = None
             for d in (0, 1):
-                tile = pieces[c, d]
-                if ez:
-                    tile = pltpu.roll(tile, 128 - EY * ez, 1)
-                tile = jnp.where(lane < EY, tile, 0.0)
+                tile = jnp.where(lane < EY, moved(pieces[c, d], -EY * ez), 0.0)
                 if d:
                     tile = pltpu.roll(tile, 1, 1)
                 sums = tile if sums is None else sums + tile
@@ -644,16 +815,25 @@
     message = placed[0]
     for zv in range(1, EZ + 1):
         rows_at, lanes_at = divmod(zv, 3)
-        tile = placed[zv]
-        if lanes_at:
-            tile = pltpu.roll(tile, (EY + 8) * lanes_at, 1)
+        tile = moved(placed[zv], (EY + 8) * lanes_at)
         if rows_at:
             tile = pltpu.roll(tile, (EX + 1) * rows_at, 0)
         message = message + tile
     rsend[...] = message
     rrecv[REACH, s] = message
     window_start(1, rsend, rrecv)
-    lax.fori_loop(NZV // 2, NZV, stencil, 0)
+
+    exchange_start(3, W.at[0])
+    lax.fori_loop(cut_a, cut_b, stencil, 0)
+    x_end(3, W.at[0])
+    inner_z(W.at[0])
+    halo_start(1, lambda x, k: V[0, x, k] + (R[0, x, k] - W[0, x, k]) * INV[0, x, k])
+    links_start(halo_links(1))
+    lax.fori_loop(cut_b, ZHI + 1, stencil, 0)
+    outer_z(3, W.at[0])
+    for x in range(NX):
+        for k in range(6):
+            V[0, x, k] = V[0, x, k] + (R[0, x, k] - W[0, x, k]) * INV[0, x, k]
 
     window_wait(1, rsend, rrecv)
 
@@ -661,9 +841,7 @@
         rows_at, lanes_at = divmod(zv, 3)
         total = None
         for t in range(n_sub):
-            tile = rrecv[o, t]
-            if lanes_at:
-                tile = pltpu.roll(tile, 128 - (EY + 8) * lanes_at, 1)
+            tile = moved(rrecv[o, t], -(EY + 8) * lanes_at)
             here = jnp.logical_and(
                 sub_i >= (EX + 1) * rows_at, sub_i < (EX + 1) * (rows_at + 1)
             )
@@ -680,27 +858,23 @@
     radius = (SPECTRUM_HIGH - SPECTRUM_LOW) / 2.0
     ratio = center / radius
     factor = 1.0 / ratio
-    for z in range(NZV):
+    for z in range(ZLO, ZHI + 1):
         o, zv = divmod(z, EZ)
-        if o == SPAN:
-            value = window_sum(o - 1, EZ)
-        else:
-            value = window_sum(o, zv)
-            if zv == 0 and o > 0:
-                value = value + window_sum(o - 1, EZ)
+        value = window_sum(o, zv)
+        if zv == 0 and o > 0:
+            value = value + window_sum(o - 1, EZ)
         CR[z] = value
         CU[0, z] = value * ST[z, 27] * (1.0 / center)
-    first, last = REACH * EZ, REACH * EZ + EZ
-    sol = [CU[0, z] for z in range(first, last + 1)]
+    first, last = FIRST - HALO, LAST_V + HALO
+    sol = {z: CU[0, z] for z in range(first, last + 1)}
     for sweep in range(CHEB_ITERS - 1):
         now, later = sweep % 2, (sweep + 1) % 2
         left = CHEB_ITERS - 2 - sweep
         nxt = 1.0 / (2.0 * ratio - factor)
-        lo, hi = max(first - left, 0), min(last + left, NZV - 1)
         wide = {}
-        for z in range(lo, hi + 1):
+        for z in range(first - left, last + left + 1):
             for zz in (z - 1, z, z + 1):
-                if zz in wide or not 0 <= zz < NZV:
+                if zz in wide:
                     continue
                 base = CU[now, zz]
                 sides = {}
@@ -711,8 +885,6 @@
                 wide[zz] = sides
             total = None
             for dz in (-1, 0, 1):
-                if not 0 <= z + dz < NZV:
-                    continue
                 for dx in (-1, 0, 1):
                     for dy in (-1, 0, 1):
                         term = ST[z, 9 * (dx + 1) + 3 * (dz + 1) + dy + 1] * wide[z + dz][dx, dy]
@@ -722,71 +894,99 @@
             fresh = (nxt * factor) * CU[now, z] + (2.0 * nxt / radius) * (residual * ST[z, 27])
             CU[later, z] = fresh
             if first <= z <= last:
-                sol[z - first] = sol[z - first] + fresh
+                sol[z] = sol[z] + fresh
         factor = nxt
 
-    own = []
-    for zv in range(EZ + 1):
-        tile = sol[zv]
-        moved = tile
+    own = {}
+    for z, tile in sol.items():
+        shifted_x = tile
         for t in range(1, n_sub):
-            moved = jnp.where(s == t, pltpu.roll(tile, (-EX * t) % xs, 0), moved)
-        own.append(moved[0:8])
-    corner_tiles = {}
-    for c in (0, 1):
-        for d in (0, 1):
-            total = None
-            for ez in range(EZ):
-                tile = own[ez + c]
-                if d:
-                    tile = pltpu.roll(tile, 127, 1)
-                tile = jnp.where(lane < EY, tile, 0.0)
-                if ez:
-                    tile = pltpu.roll(tile, EY * ez, 1)
-                total = tile if total is None else total + tile
-            corner_tiles[c, d] = total
-    spread = []
-    for xv in range(EX + 1):
-        ends = []
-        for d in (0, 1):
-            ends.append(
-                sum(
-                    LJ[c] * jnp.broadcast_to(corner_tiles[c, d][xv : xv + 1, :], (8, 128))
-                    for c in (0, 1)
-                )
-            )
-        spread.append(
-            [mac([(float(lin[k, d]), ends[d]) for d in (0, 1)]) for k in range(6)]
+            shifted_x = jnp.where(s == t, pltpu.roll(tile, (-EX * t) % xs, 0), shifted_x)
+        own[z - FIRST] = shifted_x
+
+    links_wait(halo_links(1))
+    halo_unpack(1, V.at[1])
+    for x in range(NX):
+        z0, z5 = V[0, x, :, 0, :], V[0, x, :, 5, :]
+        V[1, x, :, 5, :] = jnp.where(
+            group6 == 1, pltpu.roll(z0, EY, 1), V[1, x, :, 5, :]
         )
-    for x in range(NX):
-        ex = min(x // 5, EX - 1)
-        i = x - 5 * ex
-        for k in range(6):
-            V[x, k] = V[x, k] + mac([(float(lin[i, a]), spread[ex + a][k]) for a in (0, 1)])
-
-    for idx in (2, 3):
-        apply_part(V, W)
-        exchange_start(idx, W)
-        if idx == 2:
-            velocity(2, 0)
-            exchange_start(7, VV.at[2])
-        else:
-            for c in range(2):
-                exchange_end(5 + c, VV.at[c])
-                to_nodes(VV.at[c], velout_ref.at[c])
-        exchange_end(idx, W)
+        V[1, x, :, 0, :] = jnp.where(
+            group6 == 2, pltpu.roll(z5, 128 - EY, 1), V[1, x, :, 0, :]
+        )
+
+    ZJ = tab_ref[28]
+    for h in range(2):
+        places = range(EZ) if h == 0 else (-2, -1, EZ, EZ + 1)
+        corner_tiles = {}
+        for c in (0, 1):
+            for d in (0, 1):
+                total = None
+                for at, ez in enumerate(places):
+                    tile = own[ez + c]
+                    if d:
+                        tile = pltpu.roll(tile, 127, 1)
+                    tile = moved(jnp.where(lane[0:1] < EY, tile, 0.0), EY * at)
+                    total = tile if total is None else total + tile
+                corner_tiles[c, d] = total
+        val, zdif, ydif = {}, {}, {}
+        for xv in range(-1, EX + 2):
+            at = xv % xs
+            rows = {
+                key: jnp.broadcast_to(tile[at : at + 1, :], (8, 128))
+                for key, tile in corner_tiles.items()
+            }
+            ends = [LJ[0] * rows[0, d] + LJ[1] * rows[1, d] for d in (0, 1)]
+            val[xv] = [mac([(float(lin[k, d]), ends[d]) for d in (0, 1)]) for k in range(6)]
+            if 0 <= xv <= EX:
+                jump = [ZJ * (rows[0, d] - rows[1, d]) for d in (0, 1)]
+                zdif[xv] = [
+                    mac([(float(lin[k, d]), jump[d]) for d in (0, 1)]) for k in range(6)
+                ]
+                ydif[xv] = 0.5 * (ends[0] - ends[1])
+        for x in range(NX):
+            ex = min(x // 5, EX - 1)
+            i = x - 5 * ex
+            parts = [(float(lin[i, a]), ex + a) for a in (0, 1)]
+            gy, gz, gm = whole_geometry(h, x)
+            slope = gy * mac([(weight, ydif[xv]) for weight, xv in parts])
+            for k in range(6):
+                u = mac([(weight, val[xv][k]) for weight, xv in parts])
+                inside = gz * mac([(weight, zdif[xv][k]) for weight, xv in parts]) + gm * u
+                if x % 5 == 0:
+                    xv = x // 5
+                    inside = inside + GX[h, xv] * (0.5 * (val[xv][k] - val[xv - 1][k]))
+                    inside = inside + GX[h, xv + 1] * (0.5 * (val[xv][k] - val[xv + 1][k]))
+                value = float(w[k]) * inside
+                if k == 0:
+                    value = value + slope
+                if k == 5:
+                    value = value - slope
+                W[h, x, k] = value
+                V[h, x, k] = V[h, x, k] + u
+    fold_z(W, True)
+    for h in range(2):
+        fold_y(W.at[h])
+    for h in range(2):
         for x in range(NX):
             for k in range(6):
-                V[x, k] = V[x, k] + (R[x, k] - W[x, k]) * INV[x, k]
-    apply_part(V, W)
+                V[h, x, k] = V[h, x, k] - W[h, x, k] * INV[h, x, k]
+        apply_part(h)
+    fold_z(W, False)
+    fold_y(W.at[0])
+    x_start(6, W.at[0])
+    x_end(6, W.at[0])
+    for x in range(NX):
+        for k in range(6):
+            V[0, x, k] = V[0, x, k] + (R[0, x, k] - W[0, x, k]) * INV[0, x, k]
+    apply_part(0)
     num = jnp.zeros((8, 128), F32)
     den = jnp.zeros((8, 128), F32)
     for x in range(NX):
         for k in range(6):
-            v = V[x, k]
-            num = num + unique(x, k) * R[x, k] * v
-            den = den + v * W[x, k]
-    exchange_start(4, W)
+            v = V[0, x, k]
+            num = num + unique(x, k) * R[0, x, k] * v
+            den = den + v * W[0, x, k]
     num_row = jnp.sum(num, axis=0, keepdims=True)
     den_row = jnp.sum(den, axis=0, keepdims=True)
     num_one = jnp.sum(num_row, axis=1, keepdims=True)
@@ -806,11 +1006,14 @@
         return carry
 
     lax.fori_loop(1, n_dev, scatter, 0)
-    to_nodes(V, pres_ref)
-    exchange_end(7, VV.at[2])
-    to_nodes(VV.at[2], velout_ref.at[2])
-    exchange_end(4, W)
-    to_nodes(W, res_ref)
+    exchange_start(4, W.at[0])
+    fetch["put"].wait()
+    to_nodes(V.at[0], pres_ref)
+    for c in range(3):
+        exchange_end(c, VV.at[c])
+        to_nodes(VV.at[c], velout_ref.at[c])
+    exchange_end(4, W.at[0])
+    to_nodes(W.at[0], res_ref)
     whole = pltpu.make_async_remote_copy(
         src_ref=precv,
         dst_ref=precv,
@@ -826,8 +1029,12 @@
         pres_ref[x] = step * pres_ref[x]
         res_ref[x] = load_ref[x] - step * res_ref[x]
     whole.wait_send()
-    for idx in range(EXCH):
-        exchange_sent(idx)
+    for idx in range(5):
+        links_sent(x_links(idx) + z_links(idx))
+    for idx in range(5, EXCH):
+        links_sent(x_links(idx))
+    for idx in range(2):
+        links_sent(halo_links(idx))
     window_sent(0, csend, crecv)
     window_sent(1, rsend, rrecv)
 
@@ -847,6 +1054,7 @@
             col_tile(lin[:, 0]),
             col_tile(lin[:, 1]),
             col_tile(np.diag(k1)),
+            col_tile([0.5, 0.0, 0.0, 0.0, 0.0, -0.5]),
         ]
     )
     pick, put = pick_matrices()
@@ -861,19 +1069,27 @@
                 jax.ShapeDtypeStruct((NX, NZ, NY), F32),
                 jax.ShapeDtypeStruct((NX, NZ, NY), F32),
             ),
-            in_specs=[vm, vm, pl.BlockSpec(memory_space=pl.ANY)] + [vm] * 5,
+            in_specs=[pl.BlockSpec(memory_space=pl.ANY)] * 8,
             out_specs=(vm, vm, vm),
             scratch_shapes=[
-                pltpu.VMEM(field, F32),
-                pltpu.VMEM(field, F32),
+                pltpu.VMEM((3, NX, NZ, NY), F32),
+                pltpu.VMEM((NX, NZ, NY), F32),
+                pltpu.VMEM((3, EX * EZ * EY), F32),
+                pltpu.VMEM((1, EX * EZ * EY), F32),
+                pltpu.VMEM(tab.shape, F32),
+                pltpu.VMEM(pick.shape, BF16),
+                pltpu.VMEM(put.shape, BF16),
+                pltpu.VMEM((2,) + field, F32),
+                pltpu.VMEM((2,) + field, F32),
                 pltpu.VMEM((NX, NZP, NYP), F32),
                 pltpu.VMEM((8, EX * EZ * EY), jnp.int32),
-                pltpu.VMEM(field, F32),
-                pltpu.VMEM(field, F32),
+                pltpu.VMEM((2,) + field, F32),
+                pltpu.VMEM((2,) + field, F32),
                 pltpu.VMEM((3,) + field, F32),
                 pltpu.VMEM(field, F32),
-                pltpu.VMEM((EX, 8, 128), F32),
-                pltpu.VMEM((3, NX, 8, 128), F32),
+                pltpu.VMEM((2, EX + 2, 8, 128), F32),
+                pltpu.VMEM((2, 3, NX, 8, 128), F32),
+                pltpu.VMEM((2, 2, 3, 8, 128), F32),
                 pltpu.VMEM((4, EX, 8, 128), F32),
                 pltpu.VMEM((EXCH, 2, 6, 8, 128), F32),
                 pltpu.VMEM((EXCH, 2, 6, 8, 128), F32),
@@ -884,6 +1100,8 @@
                 pltpu.VMEM((SPAN, n_sub, 8, 128), F32),
                 pltpu.VMEM((8, 128), F32),
                 pltpu.VMEM((SPAN, n_sub, 8, 128), F32),
+                pltpu.VMEM((2, 2, ZT, 6, 8, 128), F32),
+                pltpu.VMEM((2, 2, ZT, 6, 8, 128), F32),
                 pltpu.VMEM((NZV + 1, 4, xs, 128), F32),
                 pltpu.VMEM((NZV, 28, xs, 128), F32),
                 pltpu.VMEM((2, NZV, xs, 128), F32),
@@ -894,8 +1112,10 @@
                 pltpu.SemaphoreType.DMA((EXCH, 8)),
                 pltpu.SemaphoreType.DMA((2, SPAN, n_sub)),
                 pltpu.SemaphoreType.DMA((2, SPAN, n_sub)),
+                pltpu.SemaphoreType.DMA((2, 2)),
+                pltpu.SemaphoreType.DMA((2, 2)),
                 pltpu.SemaphoreType.DMA((2,)),
-                pltpu.SemaphoreType.DMA,
+                pltpu.SemaphoreType.DMA((8,)),
             ],
             compiler_params=pltpu.CompilerParams(
                 collective_id=0, has_side_effects=True, vmem_limit_bytes=60 << 20

time: 48.2 us -> 44.5 us (0.923)
  the two profiles are of different devices: /device:TPU:0 before, /device:TPU:5 now
where the time goes in v1:
time: 44.5 us; the launch traced here: 44.3 us
  Pallas kernels  34.3 us (77%)
  local copies, waits for them, and re-layouts  9.26 us (21%)
  between operations  0.65 us (1%)
    pallas_call x1, Pallas kernels, per_device(): pl.pallas_call(functools.partial(kernel, n_blk, n_sub, xs), out_shape=(ja...  34.3 us
    reshape x3, local copies, waits for them, and re-layouts, per_device(): return (out[0].reshape(3, NLOC), out[1].reshape(NLOC), out[2].reshape(NLOC))  4.61 us
    reshape x1, local copies, waits for them, and re-layouts, per_device(): velocity.reshape(3, NX, NZ, NY)  2.69 us
    reshape x1, local copies, waits for them, and re-layouts, per_device(): pressure_load.reshape(NX, NZ, NY)  1.95 us

profile of v1, /device:TPU:5, one launch (start us, length us, event | category | flops | bytes accessed | tf_op | source)
XLA Modules:
  0.0 44.3 jit_solution(16669806242941401521)
XLA Ops:
  0.6 2.0 %reshape.25.load_hbm = f32[11,21,161]{2,1,0:T(8,128)} reshape(f32[37191]{0:T(1024)} %param.9) | data formatting | bytes 297528 | tf_op jit(solution)/shard_map/reshape | solution.py:1125
  2.6 2.7 %reshape.24.vel_hbm = f32[3,11,21,161]{3,2,1,0:T(8,128)} reshape(f32[3,37191]{1,0:T(4,128)} %param.8) | data formatting | bytes 892584 | tf_op jit(solution)/shard_map/reshape | solution.py:1124
  5.3 34.3 %shard_map.103 = (f32[3,11,21,161]{3,2,1,0:T(8,128)}, f32[11,21,161]{2,1,0:T(8,128)}, f32[11,21,161]{2,1,0:T(8,128)}) custom-call(f32[3,11,21,161]{3,2,1,0:T(8,128)} %reshape.24.vel_hbm, f32[11,21,161]{2,1,0:T(8,128)} %reshape.25.load_hbm, s32[216,256]{1,0:T(8,128)} %map_hbm.1, f32[3,256]{1,0:T(4,128)} %stiff_hbm.1, f32[1,256]{1,0:T(1,128)} %bitcast.1, ...), custom_call_target="tpu_custom_call" | custom-call | tf_op jit(solution)/shard_map/pallas_call | solution.py:1065
  39.6 0.0 copy-start.1
  39.6 2.6 %reshape.27 = f32[3,37191]{1,0:T(4,128)} reshape(f32[3,11,21,161]{3,2,1,0:T(8,128)} %get-tuple-element.6) | data formatting | bytes 892584 | tf_op jit(solution)/shard_map/reshape | solution.py:1133
  42.3 0.0 copy-done.1
  42.3 0.0 copy-start
  42.3 1.0 %reshape.28 = f32[37191]{0:T(1024)} reshape(f32[11,21,161]{2,1,0:T(8,128)S(1)} %copy-done.1) | data formatting | bytes 297528 | tf_op jit(solution)/shard_map/reshape | solution.py:1133
  43.3 0.0 copy-done
  43.3 1.0 %reshape.29 = f32[37191]{0:T(1024)} reshape(f32[11,21,161]{2,1,0:T(8,128)S(1)} %copy-done) | data formatting | bytes 297528 | tf_op jit(solution)/shard_map/reshape | solution.py:1133
Async XLA Ops:
  39.6 2.6 %copy-start.1 = (f32[11,21,161]{2,1,0:T(8,128)S(1)}, f32[11,21,161]{2,1,0:T(8,128)}, u32[]{:S(2)}) copy-start(f32[11,21,161]{2,1,0:T(8,128)} %get-tuple-element.7) | copy-start | bytes 446296
  42.3 1.0 %copy-start = (f32[11,21,161]{2,1,0:T(8,128)S(1)}, f32[11,21,161]{2,1,0:T(8,128)}, u32[]{:S(2)}) copy-start(f32[11,21,161]{2,1,0:T(8,128)} %get-tuple-element.8) | copy-start | bytes 446296

commit v2 on v1

--- a/solution.py
+++ b/solution.py
@@ -30,6 +30,17 @@
 ZHI = LAST_V + DEPTH
 EXCH = 7
 ZT = -(-NX // 4)
+ROWS = NX * NZ
+IN_STEP = next(k for k in range(1, 129) if NY * k % 128 == 127)
+IN_SKIP = (NY * IN_STEP + 1) // 128
+IN_ROWS = 8 * IN_STEP
+OUT_STEP, OUT_SKIP = next(
+    (r, p) for r in range(1, 129) for p in (NY * r // 128,) if 0 < NY * r - 128 * p <= 4
+)
+OUT_DRIFT = NY * OUT_STEP - 128 * OUT_SKIP
+FLAT = -(-NLOC // 128)
+FULL = NLOC // 1024
+PAD = 8
 LAST = (NX - 1) % 4
 
 DAMPING = 0.3
@@ -122,11 +133,22 @@
     tab_hbm,
     pick_hbm,
     put_hbm,
-    velout_ref,
-    pres_ref,
-    res_ref,
-    vel_ref,
-    load_ref,
+    velout_hbm,
+    pres_hbm,
+    res_hbm,
+    vel_flat,
+    load_flat,
+    vel_back,
+    pres_back,
+    res_back,
+    FL,
+    FI,
+    FP,
+    FR,
+    S0,
+    S1,
+    Y0,
+    Y1,
     stiff_ref,
     mass_ref,
     tab_ref,
@@ -134,7 +156,6 @@
     put_ref,
     V,
     W,
-    FS,
     map_ref,
     R,
     INV,
@@ -169,6 +190,7 @@
     h_recv,
     p_sem,
     in_sem,
+    out_sem,
 ):
     D, w, k1, lin, coarse = tables()
     Dh = bf16_round(D)
@@ -197,9 +219,11 @@
             ("stiff", stiff_hbm, stiff_ref),
             ("mass", mass_hbm, mass_ref),
             ("tab", tab_hbm, tab_ref),
-            ("load", load_hbm, load_ref),
+            ("load", load_hbm, load_flat),
             ("pick", pick_hbm, pick_ref),
-            ("vel", vel_hbm, vel_ref),
+            ("vel0", vel_hbm.at[0:1], vel_flat.at[0]),
+            ("vel1", vel_hbm.at[1:2], vel_flat.at[1]),
+            ("vel2", vel_hbm.at[2:3], vel_flat.at[2]),
             ("put", put_hbm, put_ref),
         )
     ):
@@ -245,7 +269,6 @@
             zero(rrecv.at[o])
 
     CF[...] = jnp.zeros(CF.shape, F32)
-    FS[...] = jnp.zeros(FS.shape, F32)
 
     lane = lax.broadcasted_iota(jnp.int32, (8, 128), 1)
     sub_i = lax.broadcasted_iota(jnp.int32, (8, 128), 0)
@@ -260,10 +283,84 @@
     def moved(tile, shift):
         return tile if shift % 128 == 0 else pltpu.roll(tile, shift % 128, 1)
 
-    def to_elements(field, dest, exact):
-        FS[:, 0:NZ, 0:NY] = field[...]
+    slant_in = lane - sub_i
+    slant_out = lane - OUT_DRIFT * sub_i
+
+    def spin(tile, shift, stride):
+        shift = shift % 128
+        if shift + 7 * stride > 128:
+            tile, shift = pltpu.roll(tile, shift, 1), 0
+        return pltpu.roll(tile, shift, 1, stride=stride, stride_axis=0)
+
+    chunks = [(8 * i, 8, 1024) for i in range(FULL)]
+    chunks += [(p, 1, min(128, NLOC - 128 * p)) for p in range(8 * FULL, FLAT)]
+
+    def unpack_flat(source, dest):
+        for p, n, size in chunks:
+            dest[PAD + p : PAD + p + n, 0 : size // n] = source(
+                pl.ds(128 * p, size)
+            ).reshape(n, size // n)
+
+    def pack_flat(tile, store):
+        for p, n, size in chunks:
+            store(pl.ds(128 * p, size), tile(p, n)[:, 0 : size // n])
+
+    def flat_to_rows(flat):
+        for r in range(IN_STEP):
+            q, at = divmod(NY * r, 128)
+            if at < 7:
+                q, at = q - 1, at + 128
+            a, b_, c = (
+                spin(flat[pl.ds(PAD + q + n, 8, stride=IN_SKIP), :], -at, 1) for n in range(3)
+            )
+            first_part = slant_in < 128 - at
+            if at > 128:
+                b_low = jnp.where(slant_in < 256 - at, b_, c)
+            else:
+                b_low = b_
+            S0[pl.ds(r, 8, stride=IN_STEP), :] = jnp.where(first_part, a, b_low)
+            S1[pl.ds(r, 8, stride=IN_STEP), :] = jnp.where(
+                lane < NY - 128, jnp.where(first_part, b_, c), 0.0
+            )
+
+    def rows_to_flat(dest):
+        for block in range(0, FLAT, 8 * OUT_SKIP):
+            for step in range(OUT_SKIP):
+                p = block + step
+                if p >= FLAT:
+                    continue
+                r, y = divmod(128 * p, NY)
+                if y < 7 * OUT_DRIFT:
+                    r, y = r - 1, y + NY
+
+                def piece(ref, row, turn):
+                    return spin(
+                        ref[pl.ds(PAD + row, 8, stride=OUT_STEP), :], turn, OUT_DRIFT
+                    )
+
+                value = piece(Y1, r, -y)
+                if y - 7 * OUT_DRIFT < 128:
+                    value = jnp.where(slant_out < 128 - y, piece(Y0, r, -y), value)
+                if y + 127 >= NY:
+                    after = piece(Y0, r + 1, NY - y)
+                    if y + 127 >= NY + 128:
+                        after = jnp.where(
+                            slant_out < NY + 128 - y, after, piece(Y1, r + 1, NY - y)
+                        )
+                    value = jnp.where(slant_out < NY - y, value, after)
+                dest[pl.ds(PAD + p, 8, stride=OUT_SKIP), :] = value
+
+    def to_elements(flat, dest, exact):
+        flat_to_rows(flat)
         rows = jnp.concatenate(
-            [FS[:, 5 * ez : 5 * ez + 8, :].reshape(8 * NX, NYP) for ez in range(EZ)], axis=0
+            [
+                jnp.concatenate(
+                    [S0[pl.ds(NZ * x + 5 * ez, 8), :], S1[pl.ds(NZ * x + 5 * ez, 8), :]], axis=1
+                )
+                for ez in range(EZ)
+                for x in range(NX)
+            ],
+            axis=0,
         )
         hi = rows.astype(BF16)
         got = jnp.dot(hi, pick_ref[...], preferred_element_type=F32)
@@ -289,8 +386,12 @@
             jnp.concatenate(los, axis=0).astype(BF16), put_ref[...], preferred_element_type=F32
         )
         for ez in range(EZ):
-            piece = got[8 * NX * ez : 8 * NX * (ez + 1)].reshape(NX, 8, NYP)
-            dest[:, 5 * ez : 5 * ez + 6, :] = piece[:, :6, :NY]
+            for x in range(NX):
+                at = 8 * NX * ez + 8 * x
+                row = PAD + NZ * x + 5 * ez
+                Y0[row : row + 6, :] = got[at : at + 6, 0:128]
+                Y1[row : row + 6, :] = got[at : at + 6, 128:256]
+        rows_to_flat(dest)
 
     for name in ("map", "stiff", "mass", "tab"):
         fetch[name].wait()
@@ -506,6 +607,9 @@
     def exchange_start(idx, F):
         fold_y(F)
         x_start(idx, F)
+        z_start(idx, F)
+
+    def z_start(idx, F):
         for t in range(ZT):
             low = high = jnp.zeros((6, 128), F32)
             for m in range(4):
@@ -623,7 +727,8 @@
                 copy().wait_send()
 
     def velocity(c):
-        to_elements(vel_ref.at[c], VE, False)
+        unpack_flat(lambda at: vel_flat[c, :, at], FL)
+        to_elements(FL, VE, False)
         out = VV.at[c]
         rounded = lambda value: value.astype(BF16).astype(F32)
         for ex in range(EX):
@@ -665,17 +770,22 @@
     geometry(0, stack)
     fetch["load"].wait()
     fetch["pick"].wait()
-    to_elements(load_ref, R.at[0], True)
+    unpack_flat(lambda at: load_flat[at], FI)
+    to_elements(FI, R.at[0], True)
     halo_start(0, lambda x, k: R[0, x, k])
     crecv[REACH, s] = stack
-    fetch["vel"].wait()
-
-    pl.semaphore_wait(barrier, n_dev - 1)
-
-    window_start(0, csend, crecv)
-    links_start(halo_links(0))
+    for c in range(3):
+        fetch["vel%d" % c].wait()
+
     def component(c, carry):
         velocity(c)
+
+        @pl.when(c == 0)
+        def _():
+            pl.semaphore_wait(barrier, n_dev - 1)
+            window_start(0, csend, crecv)
+            links_start(halo_links(0))
+
         exchange_start(c, VV.at[c])
         return carry
 
@@ -741,7 +851,6 @@
         return carry
 
     cut_a = ZLO + (ZHI + 1 - ZLO) // 3
-    cut_b = ZLO + (ZHI + 1 - ZLO) * 2 // 3
     lax.fori_loop(ZLO, cut_a, stencil, 0)
 
     links_wait(halo_links(0))
@@ -759,6 +868,8 @@
         for k in range(6):
             V[0, x, k] = V[0, x, k] + (R[0, x, k] - W[0, x, k]) * INV[0, x, k]
     apply_part(0)
+    fold_y(W.at[0])
+    x_start(3, W.at[0])
 
     one = jnp.ones((8, 128), F32)
     wz = jnp.where(sub_i < 5, one, 0.0)
@@ -781,7 +892,9 @@
 
     acc = [[None, None] for _ in range(EX + 1)]
     for x in range(NX):
-        rows = [unique(x, k) * R[0, x, k] - W[0, x, k] for k in range(6)]
+        rows = [unique(x, k) * R[0, x, k] - W[0, x, k] for k in range(5)]
+        last_row = unique(x, 5) * R[0, x, 5] - W[0, x, 5]
+        rows.append(jnp.where(ey == EY - 1, last_row, 0.0))
         lines = [mac([(float(lin[k, d]), rows[k]) for k in range(6)]) for d in (0, 1)]
         ex = min(x // 5, EX - 1)
         i = x - 5 * ex
@@ -823,18 +936,32 @@
     rrecv[REACH, s] = message
     window_start(1, rsend, rrecv)
 
-    exchange_start(3, W.at[0])
-    lax.fori_loop(cut_a, cut_b, stencil, 0)
+    z_start(3, W.at[0])
     x_end(3, W.at[0])
     inner_z(W.at[0])
     halo_start(1, lambda x, k: V[0, x, k] + (R[0, x, k] - W[0, x, k]) * INV[0, x, k])
     links_start(halo_links(1))
-    lax.fori_loop(cut_b, ZHI + 1, stencil, 0)
+    lax.fori_loop(cut_a, ZHI + 1, stencil, 0)
     outer_z(3, W.at[0])
     for x in range(NX):
         for k in range(6):
             V[0, x, k] = V[0, x, k] + (R[0, x, k] - W[0, x, k]) * INV[0, x, k]
 
+    fetch["put"].wait()
+
+    def velocity_out(c):
+        exchange_end(c, VV.at[c])
+        to_nodes(VV.at[c], FP)
+
+        def store(at, tile):
+            vel_back[c, :, at] = tile.reshape(1, tile.size)
+
+        pack_flat(lambda p, n: FP[PAD + p : PAD + p + n, :], store)
+        pltpu.make_async_copy(
+            vel_back.at[c], velout_hbm.at[c], out_sem.at[c]
+        ).start()
+
+    velocity_out(0)
     window_wait(1, rsend, rrecv)
 
     def window_sum(o, zv):
@@ -904,6 +1031,7 @@
             shifted_x = jnp.where(s == t, pltpu.roll(tile, (-EX * t) % xs, 0), shifted_x)
         own[z - FIRST] = shifted_x
 
+    velocity_out(1)
     links_wait(halo_links(1))
     halo_unpack(1, V.at[1])
     for x in range(NX):
@@ -1007,13 +1135,10 @@
 
     lax.fori_loop(1, n_dev, scatter, 0)
     exchange_start(4, W.at[0])
-    fetch["put"].wait()
-    to_nodes(V.at[0], pres_ref)
-    for c in range(3):
-        exchange_end(c, VV.at[c])
-        to_nodes(VV.at[c], velout_ref.at[c])
+    velocity_out(2)
+    to_nodes(V.at[0], FP)
     exchange_end(4, W.at[0])
-    to_nodes(W.at[0], res_ref)
+    to_nodes(W.at[0], FR)
     whole = pltpu.make_async_remote_copy(
         src_ref=precv,
         dst_ref=precv,
@@ -1025,9 +1150,24 @@
     whole.wait_recv()
     both = psend[...] + jnp.sum(precv[...], axis=0)
     step = both[0:1, 0:1] / both[0:1, 64:65]
-    for x in range(NX):
-        pres_ref[x] = step * pres_ref[x]
-        res_ref[x] = load_ref[x] - step * res_ref[x]
+
+    def store_to(back):
+        def store(at, tile):
+            back[at] = tile.reshape(tile.size)
+
+        return store
+
+    pack_flat(lambda p, n: step * FP[PAD + p : PAD + p + n, :], store_to(pres_back))
+    pack_flat(
+        lambda p, n: FI[PAD + p : PAD + p + n, :] - step * FR[PAD + p : PAD + p + n, :],
+        store_to(res_back),
+    )
+    backs = [
+        pltpu.make_async_copy(pres_back, pres_hbm, out_sem.at[3]),
+        pltpu.make_async_copy(res_back, res_hbm, out_sem.at[4]),
+    ]
+    for copy in backs:
+        copy.start()
     whole.wait_send()
     for idx in range(5):
         links_sent(x_links(idx) + z_links(idx))
@@ -1037,6 +1177,24 @@
         links_sent(halo_links(idx))
     window_sent(0, csend, crecv)
     window_sent(1, rsend, rrecv)
+    for c in range(3):
+        pltpu.make_async_copy(vel_back.at[c], velout_hbm.at[c], out_sem.at[c]).wait()
+    for copy in backs:
+        copy.wait()
+
+
+def place(vel_in, pres_in, res_in, vel_out, pres_out, res_out, vel, pres, res, sem):
+    pairs = [(vel_in.at[c], vel.at[c], vel_out.at[pl.ds(c, 1)]) for c in range(3)]
+    pairs += [(pres_in, pres, pres_out), (res_in, res, res_out)]
+    loads = [pltpu.make_async_copy(p[0], p[1], sem.at[0, i]) for i, p in enumerate(pairs)]
+    stores = [pltpu.make_async_copy(p[1], p[2], sem.at[1, i]) for i, p in enumerate(pairs)]
+    for copy in loads:
+        copy.start()
+    for load, store in zip(loads, stores):
+        load.wait()
+        store.start()
+    for copy in stores:
+        copy.wait()
 
 
 def solution(mesh):
@@ -1060,20 +1218,34 @@
     pick, put = pick_matrices()
 
     def per_device(velocity, pressure_load, local_map, stiff_geo, mass_geo):
-        vm = pl.BlockSpec(memory_space=pltpu.VMEM)
         field = (NX, 6, 8, 128)
+        reach_in = NY * (IN_STEP - 1) // 128 + 3 + 7 * IN_SKIP
+        reach_out = FLAT + 8 * OUT_SKIP
+        flat = pltpu.VMEM((PAD + -(-max(reach_in, reach_out) // 8) * 8, 128), F32)
+        out_rows = PAD + -(-(ROWS + 8 * OUT_STEP + 2) // 8) * 8
         out = pl.pallas_call(
             functools.partial(kernel, n_blk, n_sub, xs),
             out_shape=(
-                jax.ShapeDtypeStruct((3, NX, NZ, NY), F32),
-                jax.ShapeDtypeStruct((NX, NZ, NY), F32),
-                jax.ShapeDtypeStruct((NX, NZ, NY), F32),
+                jax.ShapeDtypeStruct((3, 1, NLOC), F32),
+                jax.ShapeDtypeStruct((NLOC,), F32),
+                jax.ShapeDtypeStruct((NLOC,), F32),
             ),
             in_specs=[pl.BlockSpec(memory_space=pl.ANY)] * 8,
-            out_specs=(vm, vm, vm),
+            out_specs=(pl.BlockSpec(memory_space=pl.ANY),) * 3,
             scratch_shapes=[
-                pltpu.VMEM((3, NX, NZ, NY), F32),
-                pltpu.VMEM((NX, NZ, NY), F32),
+                pltpu.VMEM((3, 1, NLOC), F32),
+                pltpu.VMEM((NLOC,), F32),
+                pltpu.VMEM((3, 1, NLOC), F32),
+                pltpu.VMEM((NLOC,), F32),
+                pltpu.VMEM((NLOC,), F32),
+                flat,
+                flat,
+                flat,
+                flat,
+                pltpu.VMEM((IN_ROWS, 128), F32),
+                pltpu.VMEM((IN_ROWS, 128), F32),
+                pltpu.VMEM((out_rows, 128), F32),
+                pltpu.VMEM((out_rows, 128), F32),
                 pltpu.VMEM((3, EX * EZ * EY), F32),
                 pltpu.VMEM((1, EX * EZ * EY), F32),
                 pltpu.VMEM(tab.shape, F32),
@@ -1081,7 +1253,6 @@
                 pltpu.VMEM(put.shape, BF16),
                 pltpu.VMEM((2,) + field, F32),
                 pltpu.VMEM((2,) + field, F32),
-                pltpu.VMEM((NX, NZP, NYP), F32),
                 pltpu.VMEM((8, EX * EZ * EY), jnp.int32),
                 pltpu.VMEM((2,) + field, F32),
                 pltpu.VMEM((2,) + field, F32),
@@ -1115,14 +1286,15 @@
                 pltpu.SemaphoreType.DMA((2, 2)),
                 pltpu.SemaphoreType.DMA((2, 2)),
                 pltpu.SemaphoreType.DMA((2,)),
-                pltpu.SemaphoreType.DMA((8,)),
+                pltpu.SemaphoreType.DMA((10,)),
+                pltpu.SemaphoreType.DMA((5,)),
             ],
             compiler_params=pltpu.CompilerParams(
                 collective_id=0, has_side_effects=True, vmem_limit_bytes=60 << 20
             ),
         )(
-            velocity.reshape(3, NX, NZ, NY),
-            pressure_load.reshape(NX, NZ, NY),
+            velocity,
+            pressure_load,
             local_map,
             stiff_geo,
             mass_geo.reshape(1, mass_geo.shape[0]),
@@ -1130,7 +1302,25 @@
             jnp.asarray(pick, BF16),
             jnp.asarray(put, BF16),
         )
-        return (out[0].reshape(3, NLOC), out[1].reshape(NLOC), out[2].reshape(NLOC))
+        any_spec = pl.BlockSpec(memory_space=pl.ANY)
+        return tuple(
+            pl.pallas_call(
+                place,
+                out_shape=(
+                    jax.ShapeDtypeStruct((3, NLOC), F32),
+                    jax.ShapeDtypeStruct((NLOC,), F32),
+                    jax.ShapeDtypeStruct((NLOC,), F32),
+                ),
+                in_specs=[any_spec] * 3,
+                out_specs=(any_spec,) * 3,
+                scratch_shapes=[
+                    pltpu.VMEM((3, 1, NLOC), F32),
+                    pltpu.VMEM((NLOC,), F32),
+                    pltpu.VMEM((NLOC,), F32),
+                    pltpu.SemaphoreType.DMA((2, 5)),
+                ],
+            )(*out)
+        )
 
     in_specs = (
         P(None, ("blk", "sub")),

time: 44.5 us -> 38.3 us (0.86)
  the two profiles are of different devices: /device:TPU:5 before, /device:TPU:0 now
where the time goes in v2:
time: 38.3 us; the launch traced here: 38 us
  Pallas kernels  37.2 us (97%)
  between operations  0.8 us (2%)
    pallas_call x1, Pallas kernels, per_device(): pl.pallas_call(functools.partial(kernel, n_blk, n_sub, xs), out_shape=(ja...  35.3 us
    pallas_call x1, Pallas kernels, per_device(): pl.pallas_call(place, out_shape=(jax.ShapeDtypeStruct((3, NLOC), F32), ja...  1.95 us

profile of v2, /device:TPU:0, one launch (start us, length us, event | category | flops | bytes accessed | tf_op | source)
XLA Modules:
  0.0 38.0 jit_solution(14600590602011572016)
XLA Ops:
  0.6 35.3 %shard_map.103 = (f32[3,1,37191]{2,1,0:T(1,128)}, f32[37191]{0:T(1024)}, f32[37191]{0:T(1024)}) custom-call(f32[3,37191]{1,0:T(4,128)} %vel_hbm.1, f32[37191]{0:T(1024)} %load_hbm.1, s32[216,256]{1,0:T(8,128)} %map_hbm.1, f32[3,256]{1,0:T(4,128)} %stiff_hbm.1, f32[1,256]{1,0:T(1,128)} %bitcast.1, f32[29,8,128]{2,1,0:T(8,128)} %constant.6.clone.tab_hbm, ...), custom_call_target="tpu_custom_call" | custom-call | tf_op jit(solution)/shard_map/pallas_call | solution.py:1226
  35.9 2.0 %shard_map.104 = (f32[3,37191]{1,0:T(4,128)}, f32[37191]{0:T(1024)}, f32[37191]{0:T(1024)}) custom-call(f32[3,1,37191]{2,1,0:T(1,128)} %get-tuple-element.6.vel_in, f32[37191]{0:T(1024)} %get-tuple-element.7.pres_in, f32[37191]{0:T(1024)} %get-tuple-element.8.res_in), custom_call_target="tpu_custom_call" | custom-call | tf_op jit(solution)/shard_map/pallas_call | solution.py:1307

commit v3 on v2

--- a/solution.py
+++ b/solution.py
@@ -164,6 +164,7 @@
     GX,
     GC,
     GE,
+    GP,
     SG,
     xsend,
     xrecv,
@@ -437,7 +438,10 @@
             GX[h, 1 + ex] = WJ * g[0][ex]
         for x in range(NX):
             share = [(ex, x - 5 * ex) for ex in range(EX) if 0 <= x - 5 * ex <= 5]
-            GC[h, 0, x] = WJ * mac([(float(w[i]), g[2][ex]) for ex, i in share])
+            gy = mac([(float(w[i]), g[2][ex]) for ex, i in share])
+            GC[h, 0, x] = WJ * gy
+            if h == 1:
+                GP[x] = float(w[0]) * gy
             GC[h, 1, x] = mac([(float(w[i]), g[1][ex]) for ex, i in share])
             GC[h, 2, x] = WJ * mac([(float(MASS_SHARE * w[i]), g[3][ex]) for ex, i in share])
 
@@ -496,13 +500,13 @@
                 value = value + gy * mac([(float(k1[k, m]), vs[m]) for m in range(6)])
                 dst[x, k] = dst[x, k] + value
 
-    def fold_y(F):
-        for x in range(NX):
+    def fold_y(F, planes=range(NX)):
+        for x in planes:
             low, high = F[x, 0], F[x, 5]
             F[x, 0] = low + jnp.where(ey > 0, pltpu.roll(high, 1, 1), 0.0)
             F[x, 5] = high + jnp.where(ey < EY - 1, pltpu.roll(low, 127, 1), 0.0)
 
-    def fold_z(F, both):
+    def fold_z(F):
         for x in range(NX):
             z0, z5 = F[0, x, :, 0, :], F[0, x, :, 5, :]
             h0, h5 = F[1, x, :, 0, :], F[1, x, :, 5, :]
@@ -512,11 +516,10 @@
             h0_down, h5_down = pltpu.roll(h0, 128 - EY, 1), pltpu.roll(h5, 128 - EY, 1)
             F[0, x, :, 0, :] = z0 + jnp.where(lane6 < EY, h5_down, z5_up)
             F[0, x, :, 5, :] = z5 + jnp.where(lane6 >= 128 - EY, h0_up, z0_down)
-            if both:
-                add0 = jnp.where(group6 == 2, z5_down, h5_up)
-                add5 = jnp.where(group6 == 1, z0_up, h0_down)
-                F[1, x, :, 0, :] = h0 + jnp.where(group6 == 0, 0.0, add0)
-                F[1, x, :, 5, :] = h5 + jnp.where(group6 == 3, 0.0, add5)
+            add0 = jnp.where(group6 == 2, z5_down, h5_up)
+            add5 = jnp.where(group6 == 1, z0_up, h0_down)
+            F[1, x, :, 0, :] = h0 + jnp.where(group6 == 0, 0.0, add0)
+            F[1, x, :, 5, :] = h5 + jnp.where(group6 == 3, 0.0, add5)
 
     def link(idx, slot_no, src, dst, device):
         return lambda: pltpu.make_async_remote_copy(
@@ -560,8 +563,8 @@
     def halo_links(idx):
         def one(side, device):
             return lambda: pltpu.make_async_remote_copy(
-                src_ref=bsend.at[idx, side],
-                dst_ref=brecv.at[idx, 1 - side],
+                src_ref=bsend.at[idx, side, :, :, 0:6, :],
+                dst_ref=brecv.at[idx, 1 - side, :, :, 0:6, :],
                 send_sem=h_send.at[idx, side],
                 recv_sem=h_recv.at[idx, 1 - side],
                 device_id=device,
@@ -664,13 +667,63 @@
                 bsend[idx, 0, t, k] = low
                 bsend[idx, 1, t, k] = high
 
-    def halo_unpack(idx, dst):
+    from_low = jnp.logical_and(group == 1, sub_i < 6)
+    from_high = jnp.logical_and(group == 2, sub_i < 6)
+
+    def halo_unpack(idx, store):
         for x in range(NX):
             t, m = divmod(x, 4)
             for k in range(6):
                 low = moved(brecv[idx, 0, t, k], EY - EY * m)
                 high = moved(brecv[idx, 1, t, k], 2 * EY - EY * m)
-                dst[x, k] = jnp.where(group == 1, low, jnp.where(group == 2, high, 0.0))
+                store(x, k, jnp.where(from_low, low, jnp.where(from_high, high, 0.0)))
+
+    near_rows = [
+        jnp.where(group6 == 1, float(k1[5, j]), float(k1[0, j])) for j in range(6)
+    ]
+
+    def halo_faces():
+        rims, faces = [], []
+        for x in range(NX):
+            rows = [V[1, x, :, j, :] for j in range(6)]
+            rim = jnp.where(group6 == 1, rows[5], rows[0])
+            across = mac(list(zip(near_rows, rows)))
+            rim8 = jnp.concatenate([rim, jnp.zeros((2, 128), F32)], axis=0)
+            along = CT(0) * rim8
+            for sh in range(1, 8):
+                along = along + CT(sh) * pltpu.roll(rim8, sh, 0)
+            rims.append(rim)
+            faces.append(
+                (GC[1, 1, x] * WJ)[0:6] * across
+                + GP[x, 0:6] * along[0:6]
+                + GC[1, 2, x, 0:6] * (float(w[0]) * rim)
+            )
+        for ex in range(EX):
+            scale = GX[1, 1 + ex, 0:6] * float(w[0])
+            for i in range(6):
+                x = 5 * ex + i
+                faces[x] = faces[x] + scale * mac(
+                    [(float(k1[i, m]), rims[5 * ex + m]) for m in range(6)]
+                )
+        return faces
+
+    def join_halo(F, faces, planes):
+        for x in planes:
+            z0, z5, face = F[x, :, 0, :], F[x, :, 5, :], faces[x]
+            F[x, :, 0, :] = z0 + jnp.where(
+                lane6 < EY, pltpu.roll(face, 128 - EY, 1), pltpu.roll(z5, EY, 1)
+            )
+            F[x, :, 5, :] = z5 + jnp.where(
+                lane6 >= 128 - EY, pltpu.roll(face, EY, 1), pltpu.roll(z0, 128 - EY, 1)
+            )
+        fold_y(F, planes)
+
+    def finish_apply(idx, faces):
+        F = W.at[0]
+        join_halo(F, faces, (0, NX - 1))
+        x_start(idx, F)
+        join_halo(F, faces, range(1, NX - 1))
+        x_end(idx, F)
 
     def window_copies(which, src, dst):
         out = []
@@ -805,7 +858,7 @@
     face_geometry(1, (beside(left_s) * left_on, beside(right_s) * right_on))
     for h in range(2):
         diagonal_part(h)
-    fold_z(W, True)
+    fold_z(W)
     for h in range(2):
         fold_y(W.at[h])
     for h in range(2):
@@ -814,18 +867,6 @@
                 full = W[h, x, k]
                 good = full > 0.0
                 INV[h, x, k] = jnp.where(good, DAMPING / jnp.where(good, full, 1.0), 0.0)
-
-    for o in range(SPAN):
-        for t in range(n_sub):
-            packed = crecv[o, t]
-            for ez in range(EZ):
-                if not ZLO - 1 <= EZ * o + ez <= ZHI:
-                    continue
-                tile = jnp.where(lane < EY, moved(packed, -EY * ez), 0.0)
-                for q in range(4):
-                    CF[EZ * o + ez + 1, q, EX * t : EX * t + EX, :] = tile[
-                        EX * q : EX * q + EX, :
-                    ]
 
     corners = [(a, c, d) for a in (0, 1) for c in (0, 1) for d in (0, 1)]
 
@@ -850,20 +891,17 @@
         ST[z, 27] = jnp.where(diag > 0.0, 1.0 / jnp.where(diag > 0.0, diag, 1.0), 0.0)
         return carry
 
-    cut_a = ZLO + (ZHI + 1 - ZLO) // 3
-    lax.fori_loop(ZLO, cut_a, stencil, 0)
-
+    for x in range(NX):
+        for k in range(6):
+            V[0, x, k] = R[0, x, k] * INV[0, x, k]
+    apply_part(0)
     links_wait(halo_links(0))
-    halo_unpack(0, R.at[1])
-    for h in range(2):
-        for x in range(NX):
-            for k in range(6):
-                V[h, x, k] = R[h, x, k] * INV[h, x, k]
-        apply_part(h)
-    fold_z(W, False)
-    fold_y(W.at[0])
-    x_start(5, W.at[0])
-    x_end(5, W.at[0])
+
+    def first_halo(x, k, tile):
+        V[1, x, k] = tile * INV[1, x, k]
+
+    halo_unpack(0, first_halo)
+    finish_apply(5, halo_faces())
     for x in range(NX):
         for k in range(6):
             V[0, x, k] = V[0, x, k] + (R[0, x, k] - W[0, x, k]) * INV[0, x, k]
@@ -941,7 +979,19 @@
     inner_z(W.at[0])
     halo_start(1, lambda x, k: V[0, x, k] + (R[0, x, k] - W[0, x, k]) * INV[0, x, k])
     links_start(halo_links(1))
-    lax.fori_loop(cut_a, ZHI + 1, stencil, 0)
+    for o in range(SPAN):
+        for t in range(n_sub):
+            packed = crecv[o, t]
+            for ez in range(EZ):
+                if not ZLO - 1 <= EZ * o + ez <= ZHI:
+                    continue
+                tile = jnp.where(lane < EY, moved(packed, -EY * ez), 0.0)
+                for q in range(4):
+                    CF[EZ * o + ez + 1, q, EX * t : EX * t + EX, :] = tile[
+                        EX * q : EX * q + EX, :
+                    ]
+
+    lax.fori_loop(ZLO, ZHI + 1, stencil, 0)
     outer_z(3, W.at[0])
     for x in range(NX):
         for k in range(6):
@@ -1031,9 +1081,12 @@
             shifted_x = jnp.where(s == t, pltpu.roll(tile, (-EX * t) % xs, 0), shifted_x)
         own[z - FIRST] = shifted_x
 
-    velocity_out(1)
     links_wait(halo_links(1))
-    halo_unpack(1, V.at[1])
+
+    def base_halo(x, k, tile):
+        V[1, x, k] = tile
+
+    halo_unpack(1, base_halo)
     for x in range(NX):
         z0, z5 = V[0, x, :, 0, :], V[0, x, :, 5, :]
         V[1, x, :, 5, :] = jnp.where(
@@ -1092,18 +1145,15 @@
                     value = value - slope
                 W[h, x, k] = value
                 V[h, x, k] = V[h, x, k] + u
-    fold_z(W, True)
+    fold_z(W)
     for h in range(2):
         fold_y(W.at[h])
     for h in range(2):
         for x in range(NX):
             for k in range(6):
                 V[h, x, k] = V[h, x, k] - W[h, x, k] * INV[h, x, k]
-        apply_part(h)
-    fold_z(W, False)
-    fold_y(W.at[0])
-    x_start(6, W.at[0])
-    x_end(6, W.at[0])
+    apply_part(0)
+    finish_apply(6, halo_faces())
     for x in range(NX):
         for k in range(6):
             V[0, x, k] = V[0, x, k] + (R[0, x, k] - W[0, x, k]) * INV[0, x, k]
@@ -1135,7 +1185,8 @@
 
     lax.fori_loop(1, n_dev, scatter, 0)
     exchange_start(4, W.at[0])
-    velocity_out(2)
+    for c in (1, 2):
+        velocity_out(c)
     to_nodes(V.at[0], FP)
     exchange_end(4, W.at[0])
     to_nodes(W.at[0], FR)
@@ -1254,13 +1305,14 @@
                 pltpu.VMEM((2,) + field, F32),
                 pltpu.VMEM((2,) + field, F32),
                 pltpu.VMEM((8, EX * EZ * EY), jnp.int32),
-                pltpu.VMEM((2,) + field, F32),
+                pltpu.VMEM((1,) + field, F32),
                 pltpu.VMEM((2,) + field, F32),
                 pltpu.VMEM((3,) + field, F32),
                 pltpu.VMEM(field, F32),
                 pltpu.VMEM((2, EX + 2, 8, 128), F32),
                 pltpu.VMEM((2, 3, NX, 8, 128), F32),
                 pltpu.VMEM((2, 2, 3, 8, 128), F32),
+                pltpu.VMEM((NX, 8, 128), F32),
                 pltpu.VMEM((4, EX, 8, 128), F32),
                 pltpu.VMEM((EXCH, 2, 6, 8, 128), F32),
                 pltpu.VMEM((EXCH, 2, 6, 8, 128), F32),

time: 38.3 us -> 34.2 us (0.89)
  Pallas kernels: 37.2 us -> 33.4 us
    pallas_call x1, Pallas kernels: 35.3 us -> 31.4 us  [per_device(): pl.pallas_call(functools.partial(kernel, n_blk, n_sub, xs), out_shape=(ja...]
where the time goes in v3:
time: 34.2 us; the launch traced here: 34 us
  Pallas kernels  33.4 us (98%)
  between operations  0.64 us (2%)
    pallas_call x1, Pallas kernels, per_device(): pl.pallas_call(functools.partial(kernel, n_blk, n_sub, xs), out_shape=(ja...  31.4 us
    pallas_call x1, Pallas kernels, per_device(): pl.pallas_call(place, out_shape=(jax.ShapeDtypeStruct((3, NLOC), F32), ja...  1.95 us

profile of v3, /device:TPU:0, one launch (start us, length us, event | category | flops | bytes accessed | tf_op | source)
XLA Modules:
  0.0 34.0 jit_solution(14991458602465670529)
XLA Ops:
  0.6 31.4 %shard_map.103 = (f32[3,1,37191]{2,1,0:T(1,128)}, f32[37191]{0:T(1024)}, f32[37191]{0:T(1024)}) custom-call(f32[3,37191]{1,0:T(4,128)} %vel_hbm.1, f32[37191]{0:T(1024)} %load_hbm.1, s32[216,256]{1,0:T(8,128)} %map_hbm.1, f32[3,256]{1,0:T(4,128)} %stiff_hbm.1, f32[1,256]{1,0:T(1,128)} %bitcast.1, f32[29,8,128]{2,1,0:T(8,128)} %constant.6.clone.tab_hbm, ...), custom_call_target="tpu_custom_call" | custom-call | tf_op jit(solution)/shard_map/pallas_call | solution.py:1277
  32.1 2.0 %shard_map.104 = (f32[3,37191]{1,0:T(4,128)}, f32[37191]{0:T(1024)}, f32[37191]{0:T(1024)}) custom-call(f32[3,1,37191]{2,1,0:T(1,128)} %get-tuple-element.6.vel_in, f32[37191]{0:T(1024)} %get-tuple-element.7.pres_in, f32[37191]{0:T(1024)} %get-tuple-element.8.res_in), custom_call_target="tpu_custom_call" | custom-call | tf_op jit(solution)/shard_map/pallas_call | solution.py:1359

commit v4 on v3

--- a/solution.py
+++ b/solution.py
@@ -133,14 +133,11 @@
     tab_hbm,
     pick_hbm,
     put_hbm,
-    velout_hbm,
-    pres_hbm,
-    res_hbm,
-    vel_flat,
-    load_flat,
     vel_back,
     pres_back,
     res_back,
+    vel_flat,
+    load_flat,
     FL,
     FI,
     FP,
@@ -191,7 +188,6 @@
     h_recv,
     p_sem,
     in_sem,
-    out_sem,
 ):
     D, w, k1, lin, coarse = tables()
     Dh = bf16_round(D)
@@ -1007,9 +1003,6 @@
             vel_back[c, :, at] = tile.reshape(1, tile.size)
 
         pack_flat(lambda p, n: FP[PAD + p : PAD + p + n, :], store)
-        pltpu.make_async_copy(
-            vel_back.at[c], velout_hbm.at[c], out_sem.at[c]
-        ).start()
 
     velocity_out(0)
     window_wait(1, rsend, rrecv)
@@ -1213,12 +1206,6 @@
         lambda p, n: FI[PAD + p : PAD + p + n, :] - step * FR[PAD + p : PAD + p + n, :],
         store_to(res_back),
     )
-    backs = [
-        pltpu.make_async_copy(pres_back, pres_hbm, out_sem.at[3]),
-        pltpu.make_async_copy(res_back, res_hbm, out_sem.at[4]),
-    ]
-    for copy in backs:
-        copy.start()
     whole.wait_send()
     for idx in range(5):
         links_sent(x_links(idx) + z_links(idx))
@@ -1228,22 +1215,16 @@
         links_sent(halo_links(idx))
     window_sent(0, csend, crecv)
     window_sent(1, rsend, rrecv)
-    for c in range(3):
-        pltpu.make_async_copy(vel_back.at[c], velout_hbm.at[c], out_sem.at[c]).wait()
-    for copy in backs:
-        copy.wait()
-
-
-def place(vel_in, pres_in, res_in, vel_out, pres_out, res_out, vel, pres, res, sem):
-    pairs = [(vel_in.at[c], vel.at[c], vel_out.at[pl.ds(c, 1)]) for c in range(3)]
-    pairs += [(pres_in, pres, pres_out), (res_in, res, res_out)]
-    loads = [pltpu.make_async_copy(p[0], p[1], sem.at[0, i]) for i, p in enumerate(pairs)]
-    stores = [pltpu.make_async_copy(p[1], p[2], sem.at[1, i]) for i, p in enumerate(pairs)]
-    for copy in loads:
+
+
+def place(vel, pres, res, vel_out, pres_out, res_out, sem):
+    stores = [
+        pltpu.make_async_copy(vel.at[c], vel_out.at[pl.ds(c, 1)], sem.at[c]) for c in range(3)
+    ]
+    stores.append(pltpu.make_async_copy(pres, pres_out, sem.at[3]))
+    stores.append(pltpu.make_async_copy(res, res_out, sem.at[4]))
+    for copy in stores:
         copy.start()
-    for load, store in zip(loads, stores):
-        load.wait()
-        store.start()
     for copy in stores:
         copy.wait()
 
@@ -1277,17 +1258,14 @@
         out = pl.pallas_call(
             functools.partial(kernel, n_blk, n_sub, xs),
             out_shape=(
-                jax.ShapeDtypeStruct((3, 1, NLOC), F32),
-                jax.ShapeDtypeStruct((NLOC,), F32),
-                jax.ShapeDtypeStruct((NLOC,), F32),
+                pltpu.VMEM((3, 1, NLOC), F32),
+                pltpu.VMEM((NLOC,), F32),
+                pltpu.VMEM((NLOC,), F32),
             ),
             in_specs=[pl.BlockSpec(memory_space=pl.ANY)] * 8,
-            out_specs=(pl.BlockSpec(memory_space=pl.ANY),) * 3,
+            out_specs=(pl.BlockSpec(memory_space=pltpu.VMEM),) * 3,
             scratch_shapes=[
                 pltpu.VMEM((3, 1, NLOC), F32),
-                pltpu.VMEM((NLOC,), F32),
-                pltpu.VMEM((3, 1, NLOC), F32),
-                pltpu.VMEM((NLOC,), F32),
                 pltpu.VMEM((NLOC,), F32),
                 flat,
                 flat,
@@ -1339,7 +1317,6 @@
                 pltpu.SemaphoreType.DMA((2, 2)),
                 pltpu.SemaphoreType.DMA((2,)),
                 pltpu.SemaphoreType.DMA((10,)),
-                pltpu.SemaphoreType.DMA((5,)),
             ],
             compiler_params=pltpu.CompilerParams(
                 collective_id=0, has_side_effects=True, vmem_limit_bytes=60 << 20
@@ -1363,15 +1340,10 @@
                     jax.ShapeDtypeStruct((NLOC,), F32),
                     jax.ShapeDtypeStruct((NLOC,), F32),
                 ),
-                in_specs=[any_spec] * 3,
+                in_specs=[pl.BlockSpec(memory_space=pltpu.VMEM)] * 3,
                 out_specs=(any_spec,) * 3,
-                scratch_shapes=[
-                    pltpu.VMEM((3, 1, NLOC), F32),
-                    pltpu.VMEM((NLOC,), F32),
-                    pltpu.VMEM((NLOC,), F32),
-                    pltpu.SemaphoreType.DMA((2, 5)),
-                ],
-            )(*out)
+                scratch_shapes=[pltpu.SemaphoreType.DMA((5,))],
+            )(*(pltpu.with_memory_space_constraint(o, pltpu.VMEM) for o in out))
         )
 
     in_specs = (

time: 34.2 us -> 32.5 us (0.950)
  Pallas kernels: 33.4 us -> 31.7 us
    pallas_call x1, Pallas kernels: 1.95 us -> 0.91 us  [per_device(): pl.pallas_call(place, out_shape=(jax.ShapeDtypeStruct((3, NLOC), F32), ja...]
    pallas_call x1, Pallas kernels: 31.4 us -> 30.8 us  [per_device(): pl.pallas_call(functools.partial(kernel, n_blk, n_sub, xs), out_shape=(pl...]
where the time goes in v4:
time: 32.5 us; the launch traced here: 32.3 us
  Pallas kernels  31.7 us (98%)
  between operations  0.64 us (2%)
    pallas_call x1, Pallas kernels, per_device(): pl.pallas_call(functools.partial(kernel, n_blk, n_sub, xs), out_shape=(pl...  30.8 us
    pallas_call x1, Pallas kernels, per_device(): pl.pallas_call(place, out_shape=(jax.ShapeDtypeStruct((3, NLOC), F32), ja...  0.91 us

profile of v4, /device:TPU:0, one launch (start us, length us, event | category | flops | bytes accessed | tf_op | source)
XLA Modules:
  0.0 32.3 jit_solution(7016427584807441556)
XLA Ops:
  0.6 30.8 %shard_map.103 = (f32[3,1,37191]{2,1,0:T(1,128)S(1)}, f32[37191]{0:T(1024)S(1)}, f32[37191]{0:T(1024)S(1)}) custom-call(f32[3,37191]{1,0:T(4,128)} %vel_hbm.1, f32[37191]{0:T(1024)} %load_hbm.1, s32[216,256]{1,0:T(8,128)} %map_hbm.1, f32[3,256]{1,0:T(4,128)} %stiff_hbm.1, f32[1,256]{1,0:T(1,128)} %bitcast.1, f32[29,8,128]{2,1,0:T(8,128)} %constant.6.clone.tab_hbm, ...), custom_call_target="tpu_custom_call" | custom-call | tf_op jit(solution)/shard_map/pallas_call | solution.py:1258
  31.4 0.9 %shard_map.104 = (f32[3,37191]{1,0:T(4,128)}, f32[37191]{0:T(1024)}, f32[37191]{0:T(1024)}) custom-call(f32[3,1,37191]{2,1,0:T(1,128)S(1)} %get-tuple-element.6.vel, f32[37191]{0:T(1024)S(1)} %get-tuple-element.7.pres, f32[37191]{0:T(1024)S(1)} %get-tuple-element.8.res), custom_call_target="tpu_custom_call" | custom-call | tf_op jit(solution)/shard_map/pallas_call | solution.py:1336
